TPU v7x, 32 devices: a whole 2x2x4 slice. The times are simulated.
32 devices in a mesh: frame: 16 (over z, y, core), head: 2 (over x).
Axes of the slice: x: 2, y: 2, z: 4, core: 2. Of those that a mesh axis runs over, the one named last changes fastest.
Arguments:
- tokens: bfloat16 [16384, 3072], P('frame'), may hold values from -6 to 6
- qkv_weight: bfloat16 [3, 3072, 3072], P(None, None, 'head'), may hold values from -0.109375 to 0.109375
- query_gain: float32 [128], replicated, may hold values from 0.1 to 1.9
- key_gain: float32 [128], replicated, may hold values from 0.1 to 1.9
- labels: int32 [24], P('head'), may hold values from 0 to 1, as said below
- space_mask: int32 [24, 16, 48], P('head'), may hold values from 0 to 1, as said below
- time_mask: int32 [24, 2, 2], P('head'), may hold values from 0 to 1, as said below
Outputs:
- attended: bfloat16 [16384, 3072], P(('frame', 'head'))
Inputs may be any that keep to these rules, and one draw needn't show every extreme that they name: `labels`: among heads 3 * j, 3 * j + 1 and 3 * j + 2 exactly one is temporal. space_mask[h, a, 16 + a] = 1 for every head and query block. For each head, at most 8 key blocks of the previous frame (b < 16) are allowed for some query block, and at most 8 of the next frame (b >= 32); some head reaches 8 on each side. time_mask[h, a, a] = 1 for every head and query block.
All inputs are finite; a program needn't handle non-finite values.
Results may differ from a plain program's by a relative error of at most 0.0073.
Values may be sent and summed in bfloat16 or wider, within the bound.
A program may use at most 192 MiB of HBM per device.

v0:
```python
import math

import jax
import jax.numpy as jnp
from jax import lax
from jax.sharding import PartitionSpec as P

STRIP = 8
BLOCK = 64


epsilon = 1e-06


def padded(cells, sides, width):
    for axis, dim in sides:
        count = lax.axis_size(axis)
        ends = count - 1
        head = lax.slice_in_dim(cells, 0, width, axis=dim)
        tail = lax.slice_in_dim(cells, cells.shape[dim] - width, cells.shape[dim], axis=dim)
        cells = jnp.concatenate(
            [
                lax.ppermute(tail, axis, [(i, (i + 1) % count) for i in range(ends)]),
                cells,
                lax.ppermute(head, axis, [((i + 1) % count, i) for i in range(ends)]),
            ],
            axis=dim,
        )
    return cells


def normed(projected, gains):
    inverse_rms = lax.rsqrt(jnp.mean(projected * projected, axis=-1, keepdims=True) + epsilon)
    return (projected * inverse_rms * gains).astype(jnp.bfloat16)


def weigh(scores, column_mask):
    shape = scores.shape
    parts = scores.reshape(shape[:-2] + (shape[-2] // BLOCK, BLOCK, shape[-1]))
    weight = jnp.exp(parts) * column_mask[..., :, None, :]
    weight = weight.reshape(shape)
    denominator = jnp.sum(weight, axis=-1, keepdims=True)
    return (weight.astype(jnp.bfloat16), denominator)


def send_strips(packed):
    return lax.all_to_all(packed, "frame", split_axis=1, concat_axis=1, tiled=True)


def on_device(tokens, qkv_weight, query_gain, key_gain, labels, space_mask, time_mask):
    frame_count = lax.axis_size("frame")
    own_index = lax.axis_index("frame")
    row_count = tokens.shape[0]
    local_heads = labels.shape[0]
    head_dim = query_gain.shape[0]
    groups = local_heads // 3
    blocks = row_count // BLOCK
    space_count = 2 * groups
    scale = 1.0 / math.sqrt(head_dim)
    picked = labels.reshape(groups, 3)
    time_slot = jnp.sum(picked * jnp.arange(3, dtype=jnp.int32)[None, :], axis=1)
    group_base = 3 * jnp.arange(groups, dtype=jnp.int32)
    time_heads = group_base + time_slot
    first_space = group_base + jnp.where(time_slot == 0, 1, 0)
    second_space = group_base + jnp.where(time_slot == 2, 1, 2)
    space_heads = jnp.stack([first_space, second_space], axis=1).reshape(space_count)
    projected = jnp.einsum("td,kdc->ktc", tokens, qkv_weight, preferred_element_type=jnp.float32)
    projected = projected.reshape(3, row_count, local_heads, head_dim)
    queries = normed(projected[0], query_gain)
    key_rows = normed(projected[1], key_gain)
    values = projected[2].astype(jnp.bfloat16)
    space_q = jnp.take(queries, space_heads, axis=1)
    space_k = jnp.take(key_rows, space_heads, axis=1)
    space_v = jnp.take(values, space_heads, axis=1)
    time_q = jnp.take(queries, time_heads, axis=1)
    time_k = jnp.take(key_rows, time_heads, axis=1)
    time_v = jnp.take(values, time_heads, axis=1)
    packed = jnp.stack([time_q, time_k, time_v])
    space_live = jnp.take(space_mask, space_heads, axis=0)
    lower_ok = (own_index > 0).astype(jnp.float32)
    upper_ok = (own_index < frame_count - 1).astype(jnp.float32)
    own_pair = jnp.stack([space_k, space_v]).reshape(2, row_count, space_count * head_dim)
    near_pair = padded(own_pair, (("frame", 1),), row_count)
    reach = jnp.concatenate(
        [
            jnp.ones((blocks,), jnp.float32) * lower_ok,
            jnp.ones((blocks,), jnp.float32),
            jnp.ones((blocks,), jnp.float32) * upper_ok,
        ]
    )
    allowed_blocks = space_live.astype(jnp.float32) * reach[None, None, :]
    received = send_strips(packed)
    key_total = near_pair.shape[1]
    near_keys = near_pair[0].reshape(key_total, space_count, head_dim)
    near_values = near_pair[1].reshape(key_total, space_count, head_dim)
    space_scores = (
        jnp.einsum("rhd,chd->hrc", space_q, near_keys, preferred_element_type=jnp.float32) * scale
    )
    column_mask = jnp.repeat(allowed_blocks, BLOCK, axis=-1)
    space_weight, space_total = weigh(space_scores, column_mask)
    space_mixed = jnp.einsum(
        "hrc,chd->rhd", space_weight, near_values, preferred_element_type=jnp.float32
    )
    space_out = (space_mixed / jnp.transpose(space_total, (1, 0, 2))).astype(jnp.bfloat16)
    pos_count = row_count // frame_count
    strip_count = pos_count // STRIP
    strip_length = frame_count * STRIP
    strips = received.reshape(3, frame_count, strip_count, STRIP, groups, head_dim)
    strips = strips.transpose(0, 4, 2, 1, 3, 5).reshape(
        3, groups, strip_count, strip_length, head_dim
    )
    time_columns = jnp.repeat(
        jnp.take(time_mask, time_heads, axis=0).astype(jnp.float32), BLOCK, axis=-1
    )[:, None]
    time_scores = (
        jnp.einsum("gsrd,gscd->gsrc", strips[0], strips[1], preferred_element_type=jnp.float32)
        * scale
    )
    time_weight, time_total = weigh(time_scores, time_columns)
    time_mixed = jnp.einsum(
        "gsrc,gscd->gsrd", time_weight, strips[2], preferred_element_type=jnp.float32
    )
    time_result = (time_mixed / time_total).astype(jnp.bfloat16)
    returning = time_result.reshape(groups, strip_count, frame_count, STRIP, head_dim)
    returning = returning.transpose(2, 1, 3, 0, 4).reshape(row_count, groups, head_dim)
    time_out = lax.all_to_all(returning, "frame", split_axis=0, concat_axis=0, tiled=True)
    merged = jnp.concatenate([space_out, time_out], axis=1)
    order_all = jnp.concatenate([space_heads, time_heads])
    head_ids = jnp.arange(local_heads, dtype=jnp.int32)
    inverse = jnp.sum(
        head_ids[:, None] * (order_all[:, None] == head_ids[None, :]).astype(jnp.int32), axis=0
    )
    result = jnp.take(merged, inverse, axis=1).reshape(row_count, local_heads * head_dim)
    return lax.all_to_all(result, "head", split_axis=0, concat_axis=1, tiled=True)


def solution(mesh):
    placed = (
        P("frame", None),
        P(None, None, "head"),
        P(),
        P(),
        P("head"),
        P("head", None, None),
        P("head", None, None),
    )
    return jax.shard_map(
        on_device, mesh=mesh, in_specs=placed, out_specs=P(("frame", "head"), None), check_vma=False
    )
```

profile of v0, /device:TPU:18, one launch (start us, length us, event | category | flops | bytes accessed | tf_op | source)
XLA Modules:
  0.0 341.3 jit_solution(14805275672358833437)
XLA Ops:
  0.0 37.4 %convolution_bitcast_fusion = f32[3,1024,1536]{1,2,0:T(8,128)} fusion(bf16[3,3072,1536]{2,1,0:T(8,128)(2,1)} %param.12, bf16[1024,3072]{1,0:T(8,128)(2,1)} %param.11), kind=kOutput, calls=%fused_computation.13 | convolution fusion | flops 28991029248 | bytes 53477376 | tf_op jit(solution)/shard_map/td,kdc->ktc/dot_general | solution.py:67
  37.4 12.0 %fusion.29 = (f32[1,1024,1536]{1,2,0:T(8,128)}, f32[1,1024,1536]{1,2,0:T(8,128)}) fusion(f32[3,1024,1536]{1,2,0:T(8,128)} %convolution_bitcast_fusion), kind=kLoop, calls=%fused_computation.87 | loop fusion | bytes 25165824 | tf_op jit(solution)/shard_map/slice | solution.py:69
  49.3 6.6 %copy.86 = f32[1024,12,128]{2,0,1:T(8,128)} copy(f32[1024,12,128]{0,2,1:T(8,128)} %bitcast.104) | data formatting | bytes 12582912 | tf_op jit(solution)/shard_map/squeeze | solution.py:70
  56.0 3.6 %multiply_reduce_fusion.1 = f32[1024,12]{0,1:T(8,128)S(1)} fusion(f32[1024,12,128]{0,2,1:T(8,128)} %bitcast.105), kind=kLoop, calls=%fused_computation.19 | loop fusion | flops 3133440 | bytes 6340608 | tf_op jit(solution)/shard_map/reduce_sum | solution.py:33
  59.6 3.3 slice.66
  63.4 2.0 gather_fusion.4
  65.4 6.1 %multiply_convert_fusion.1 = bf16[1024,12,128]{2,0,1:T(8,128)(2,1)} fusion(f32[1024,12,128]{2,0,1:T(8,128)} %copy.86, f32[128]{0:T(128)S(1)} %copy-done.6, f32[1024,12]{0,1:T(8,128)S(1)} %add_rsqrt_fusion.1), kind=kLoop, calls=%fused_computation.18 | loop fusion | flops 4718592 | bytes 9486848 | tf_op jit(solution)/shard_map/convert_element_type | solution.py:34
  71.5 4.1 %gather_fusion.3 = bf16[8,1024,128]{2,1,0:T(8,128)(2,1)} fusion(bf16[1024,12,128]{2,0,1:T(8,128)(2,1)} %multiply_convert_fusion.1, s32[1024]{0:T(1024)S(1)} %pad_clamp_fusion.4), kind=kCustom, calls=%fused_computation.clone | custom fusion | bytes 4194336 | tf_op jit(solution)/shard_map/jit(_take)/gather | solution.py:73
  75.6 3.3 broadcast_select_fusion
  78.9 1.6 select_bitcast_fusion
  80.5 3.9 %copy.87 = bf16[1024,8,128]{0,2,1:T(8,128)(2,1)} copy(bf16[1024,8,128]{2,0,1:T(8,128)(2,1)} %select_bitcast_fusion) | data formatting | bytes 4194304 | tf_op jit(solution)/shard_map/jit(_take)/select_n | solution.py:73
  84.4 4.6 %pad_maximum_fusion.1 = bf16[2,1024,1024]{1,2,0:T(8,128)(2,1)} fusion(bf16[1,1024,1024]{1,2,0:T(8,128)(2,1)} %bitcast.109, bf16[1,1024,1024]{1,2,0:T(8,128)(2,1)} %bitcast.111), kind=kLoop, calls=%fused_computation.20 | loop fusion | flops 2097152 | bytes 8388608 | tf_op jit(solution)/shard_map/stack | solution.py:82
  88.9 2.7 collective-permute-start.1
  91.7 1.9 collective-permute-start
  93.6 6.6 %copy.88 = f32[1024,12,128]{2,0,1:T(8,128)} copy(f32[1024,12,128]{0,2,1:T(8,128)} %bitcast.102) | data formatting | bytes 12582912 | tf_op jit(solution)/shard_map/squeeze | solution.py:69
  100.2 3.6 %multiply_reduce_fusion = f32[1024,12]{0,1:T(8,128)S(1)} fusion(f32[1024,12,128]{0,2,1:T(8,128)} %bitcast.103), kind=kLoop, calls=%fused_computation.17 | loop fusion | flops 3133440 | bytes 6340608 | tf_op jit(solution)/shard_map/reduce_sum | solution.py:33
  103.9 2.8 copy.91
  106.7 3.6 %gather_fusion.7 = bf16[4,1024,128]{2,1,0:T(8,128)(2,1)} fusion(bf16[1024,12,128]{2,0,1:T(8,128)(2,1)} %multiply_convert_fusion.1, s32[1024]{0:T(1024)S(1)} %pad_clamp_fusion.2), kind=kCustom, calls=%fused_computation.4.clone | custom fusion | bytes 2097168 | tf_op jit(solution)/shard_map/jit(_take)/gather | solution.py:76
  110.3 4.4 %multiply_convert_fusion = bf16[1024,12,128]{2,0,1:T(8,128)(2,1)S(1)} fusion(f32[1024,12,128]{2,0,1:T(8,128)} %copy.88, f32[128]{0:T(128)S(1)} %copy-done.7, f32[1024,12]{0,1:T(8,128)S(1)} %add_rsqrt_fusion), kind=kLoop, calls=%fused_computation.16 | loop fusion | flops 4718592 | bytes 9486848 | tf_op jit(solution)/shard_map/convert_element_type | solution.py:34
  114.7 1.7 gather_fusion.6
  116.4 3.6 %gather_fusion.8 = bf16[4,1024,128]{2,1,0:T(8,128)(2,1)} fusion(bf16[1024,12,128]{2,0,1:T(8,128)(2,1)} %copy.91, s32[1024]{0:T(1024)S(1)} %pad_clamp_fusion.2), kind=kCustom, calls=%fused_computation.5.clone | custom fusion | bytes 2097168 | tf_op jit(solution)/shard_map/jit(_take)/gather | solution.py:77
  119.9 2.2 select_bitcast_fusion.3
  122.5 4.1 %copy.92 = bf16[3,1024,4,128]{3,2,0,1:T(4,128)(2,1)} copy(bf16[3,1024,4,128]{3,1,2,0:T(8,128)(2,1)S(1)} %pad_maximum_fusion.2) | data formatting | bytes 6291456 | tf_op jit(solution)/shard_map/stack | solution.py:78
  126.5 7.8 %all-to-all-start = ((bf16[3,1024,4,128]{3,2,0,1:T(4,128)(2,1)}), bf16[3,1024,4,128]{3,2,0,1:T(4,128)(2,1)}, u32[]{:S(2)}, u32[]{:S(2)}) async-start(bf16[3,1024,4,128]{3,2,0,1:T(4,128)(2,1)} %copy.92), calls=%async_computation | async-start | bytes 6291456 | tf_op jit(solution)/shard_map/all_to_all | solution.py:47
  134.5 2.2 gather_fusion.5
  136.8 0.6 gather_fusion.1
  138.5 2.1 broadcast_in_dim.81
  140.7 3.4 mul.164
  144.3 11.7 %collective-permute-done.1 = bf16[2,1024,1024]{1,2,0:T(8,128)(2,1)} collective-permute-done((bf16[2,1024,1024]{1,2,0:T(8,128)(2,1)}, bf16[2,1024,1024]{1,2,0:T(8,128)(2,1)}, u32[]{:S(2)}, u32[]{:S(2)}) %collective-permute-start.1) | collective-permute-done | bytes 4194336 | tf_op jit(solution)/shard_map/ppermute | solution.py:25
  156.1 4.6 %collective-permute-done = bf16[2,1024,1024]{1,2,0:T(8,128)(2,1)} collective-permute-done((bf16[2,1024,1024]{1,2,0:T(8,128)(2,1)}, bf16[2,1024,1024]{1,2,0:T(8,128)(2,1)}, u32[]{:S(2)}, u32[]{:S(2)}) %collective-permute-start) | collective-permute-done | bytes 4194336 | tf_op jit(solution)/shard_map/ppermute | solution.py:23
  160.7 6.0 %pad_maximum_fusion = bf16[2,3072,1024]{1,2,0:T(8,128)(2,1)S(1)} fusion(bf16[2,1024,1024]{1,2,0:T(8,128)(2,1)} %collective-permute-done.1, bf16[1,1024,1024]{1,2,0:T(8,128)(2,1)S(1)} %bitcast.110, bf16[1,1024,1024]{1,2,0:T(8,128)(2,1)} %bitcast.112, bf16[2,1024,1024]{1,2,0:T(8,128)(2,1)} %collective-permute-done), kind=kLoop, calls=%fused_computation.12 | loop fusion | flops 50331648 | bytes 25165824 | tf_op jit(solution)/shard_map/concatenate | solution.py:21
  166.7 3.7 %fusion.30 = (bf16[1,3072,1024]{1,2,0:T(8,128)(2,1)S(1)}, bf16[1,3072,1024]{1,2,0:T(8,128)(2,1)}) fusion(bf16[2,3072,1024]{1,2,0:T(8,128)(2,1)S(1)} %pad_maximum_fusion), kind=kLoop, calls=%fused_computation.88 | loop fusion | bytes 25165824 | tf_op jit(solution)/shard_map/slice | solution.py:94
  170.4 26.0 %fusion = (f32[8,1024]{1,0:T(8,128)S(1)}, bf16[8,1024,3072]{2,1,0:T(8,128)(2,1)}) fusion(f32[8,16,3072]{2,1,0:T(8,128)S(1)} %copy-done.4, bf16[3072,8,128]{0,2,1:T(8,128)(2,1)S(1)} %bitcast.106, bf16[8,1024,128]{2,1,0:T(8,128)(2,1)} %gather_fusion.5, pred[8]{0:T(512)(128)(4,1)S(1)} %compare_and_fusion.1), kind=kOutput, calls=%fused_computation.10 | convolution fusion | flops 6544154624 | bytes 60325896 | tf_op jit(solution)/shard_map/rhd,chd->hrc/dot_general | solution.py:97
  196.4 19.3 %all-to-all-done = bf16[3,1024,4,128]{3,2,0,1:T(4,128)(2,1)} async-done(((bf16[3,1024,4,128]{3,2,0,1:T(4,128)(2,1)}), bf16[3,1024,4,128]{3,2,0,1:T(4,128)(2,1)}, u32[]{:S(2)}, u32[]{:S(2)}) %all-to-all-start) | async-done | bytes 3145760 | tf_op jit(solution)/shard_map/all_to_all | solution.py:47
  215.7 2.4 copy.93
  218.1 0.7 fusion.31
  218.8 0.9 fusion.8
  219.7 1.2 fusion.10
  221.2 1.8 copy.101
  223.0 39.6 %all-to-all-start.1 = ((bf16[1024,4,128]{2,1,0:T(4,128)(2,1)}), bf16[1024,4,128]{2,1,0:T(4,128)(2,1)S(1)}, u32[]{:S(2)}, u32[]{:S(2)}) async-start(bf16[1024,4,128]{2,1,0:T(4,128)(2,1)} %copy.101), calls=%async_computation.1 | async-start | bytes 2097152 | tf_op jit(solution)/shard_map/all_to_all | solution.py:126
  262.6 25.2 %fusion.3 = bf16[1024,8,128]{0,2,1:T(8,128)(2,1)} fusion(bf16[3072,8,128]{0,2,1:T(8,128)(2,1)} %bitcast.116, bf16[8,1024,3072]{2,1,0:T(8,128)(2,1)} %get-tuple-element.10, f32[1024,8]{0,1:T(8,128)S(1)} %bitcast.119), kind=kOutput, calls=%fused_computation.22 | convolution fusion | flops 6444548096 | bytes 58753024 | tf_op jit(solution)/shard_map/hrc,chd->rhd/dot_general | solution.py:101
  287.9 1.5 copy.102
  289.4 2.2 pad_maximum_fusion.3
  291.6 2.5 gather_fusion.2
  294.1 4.8 %gather.23 = bf16[2,512,1536]{1,0,2:T(2,128)(2,1)S(1)} reshape(bf16[1024,12,128]{0,2,1:T(8,128)(2,1)} %bitcast.113) | data formatting | bytes 6291456 | tf_op jit(solution)/shard_map/jit(_take)/gather | solution.py:133
  298.9 1.3 copy_select_fusion
  300.2 38.1 %all_to_all.26 = bf16[2,512,1536]{1,2,0:T(8,128)(2,1)S(1)} all-to-all(bf16[2,512,1536]{1,2,0:T(8,128)(2,1)S(1)} %copy_select_fusion), channel_id=1, replica_groups=mesh['frame'=16,'head'=2] {'head'}, dimensions={0} | all-to-all | bytes 6291456 | tf_op jit(solution)/shard_map/all_to_all | solution.py:134
  338.2 3.0 copy.104
  (57 shorter events, 2.7 us)
Async XLA Ops:
  0.0 137.8 %copy-start = (s32[12,16,48]{2,1,0:T(8,128)S(1)}, s32[12,16,48]{2,1,0:T(8,128)}, u32[]{:S(2)}) copy-start(s32[12,16,48]{2,1,0:T(8,128)} %param.16) | copy-start | bytes 110596
  59.6 3.3 copy-start.8
  62.9 2.5 copy-start.6
  75.6 3.3 copy-start.3
  88.9 67.1 %collective-permute-start.1 = (bf16[2,1024,1024]{1,2,0:T(8,128)(2,1)}, bf16[2,1024,1024]{1,2,0:T(8,128)(2,1)}, u32[]{:S(2)}, u32[]{:S(2)}) collective-permute-start(bf16[2,1024,1024]{1,2,0:T(8,128)(2,1)} %pad_maximum_fusion.1), channel_id=1, source_target_pairs={{2,0},{4,2},{6,4},{8,6},{10,8},{12,10},{14,12},{16,14},{18,16},{20... | collective-permute-start | bytes 12582920 | tf_op jit(solution)/shard_map/ppermute | solution.py:25
  91.7 69.0 %collective-permute-start = (bf16[2,1024,1024]{1,2,0:T(8,128)(2,1)}, bf16[2,1024,1024]{1,2,0:T(8,128)(2,1)}, u32[]{:S(2)}, u32[]{:S(2)}) collective-permute-start(bf16[2,1024,1024]{1,2,0:T(8,128)(2,1)} %pad_maximum_fusion.1), channel_id=1, source_target_pairs={{0,2},{2,4},{4,6},{6,8},{8,10},{10,12},{12,14},{14,16},{16,18},{18... | collective-permute-start | bytes 12582920 | tf_op jit(solution)/shard_map/ppermute | solution.py:23
  103.8 6.4 %copy-start.7 = (f32[128]{0:T(128)S(1)}, f32[128]{0:T(128)}, u32[]{:S(2)}) copy-start(f32[128]{0:T(128)} %param.13) | copy-start | bytes 1540
  126.5 89.1 %all-to-all-start = ((bf16[3,1024,4,128]{3,2,0,1:T(4,128)(2,1)}), bf16[3,1024,4,128]{3,2,0,1:T(4,128)(2,1)}, u32[]{:S(2)}, u32[]{:S(2)}) async-start(bf16[3,1024,4,128]{3,2,0,1:T(4,128)(2,1)} %copy.92), calls=%async_computation | async-start | bytes 6291456 | tf_op jit(solution)/shard_map/all_to_all | solution.py:47
  134.4 2.3 copy-start.5
  140.7 20.0 %copy-start.2 = (bf16[8,1024,128]{1,2,0:T(8,128)(2,1)S(1)}, bf16[8,1024,128]{1,2,0:T(8,128)(2,1)}, u32[]{:S(2)}) copy-start(bf16[8,1024,128]{1,2,0:T(8,128)(2,1)} %broadcast_select_fusion) | copy-start | bytes 6291460
  166.7 3.7 %copy-start.4 = (f32[8,16,3072]{2,1,0:T(8,128)S(1)}, f32[8,16,3072]{2,1,0:T(8,128)}, u32[]{:S(2)}) copy-start(f32[8,16,3072]{2,1,0:T(8,128)} %mul.164) | copy-start | bytes 4718596
  223.0 64.9 %all-to-all-start.1 = ((bf16[1024,4,128]{2,1,0:T(4,128)(2,1)}), bf16[1024,4,128]{2,1,0:T(4,128)(2,1)S(1)}, u32[]{:S(2)}, u32[]{:S(2)}) async-start(bf16[1024,4,128]{2,1,0:T(4,128)(2,1)} %copy.101), calls=%async_computation.1 | async-start | bytes 2097152 | tf_op jit(solution)/shard_map/all_to_all | solution.py:126
  338.2 3.0 copy-start.1
where the time goes:
time: 345 us; the launch traced here: 341 us
  matrix products  90.6 us (26%)
  local copies, waits for them, and re-layouts  84.5 us (24%)
  starting transfers between devices  52.1 us (15%)
  other arithmetic  40 us (12%)
  blocking collectives  38.1 us (11%)
  waiting for transfers between devices  35.6 us (10%)
    all_to_all x1, starting transfers between devices, on_device(): lax.all_to_all(returning, 'frame', split_axis=0, concat_axis=0, tiled=True)  39.6 us
    all_to_all x1, blocking collectives, on_device(): lax.all_to_all(result, 'head', split_axis=0, concat_axis=1, tiled=True)  38.1 us
    dot_general x1, matrix products, on_device(): jnp.einsum('td,kdc->ktc', tokens, qkv_weight, preferred_element_type=jnp....  37.4 us
    dot_general x1, matrix products, on_device(): jnp.einsum('rhd,chd->hrc', space_q, near_keys, preferred_element_type=jnp...  26 us
    dot_general x1, matrix products, on_device(): jnp.einsum('hrc,chd->rhd', space_weight, near_values, preferred_element_t...  25.2 us
    all_to_all x1, waiting for transfers between devices, send_strips(): lax.all_to_all(packed, 'frame', split_axis=1, concat_axis=1, tiled=True)  19.3 us
    slice x1, local copies, waits for them, and re-layouts, on_device(): queries = normed(projected[0], query_gain)  12 us
    ppermute x1, waiting for transfers between devices, padded(): lax.ppermute(head, axis, [((i + 1) % count, i) for i in range(ends)])  11.7 us
  transfers between devices with their start and end apart: 4, of which 3 were waited for; matrix products, arithmetic and copies ran while one was open for 30% of the time, Pallas kernels for 0%

commit v1 on v0

v1 whole, which is shorter than its diff:
```python
import functools
import math

import jax
import jax.numpy as jnp
from jax import lax
from jax.experimental import pallas as pl
from jax.experimental.pallas import tpu as pltpu
from jax.sharding import PartitionSpec as P

STRIP = 8
BLOCK = 64
NEAR_MAX = 8
HD = 128
epsilon = 1e-06
BIG = 1e30
VMEM_LIMIT = 56 * 1024 * 1024


def chunk_rows(rows, want):
    while rows % want:
        want //= 2
    return want


def normed_head(projected, gains):
    inverse_rms = lax.rsqrt(jnp.mean(projected * projected, axis=-1, keepdims=True) + epsilon)
    return (projected * inverse_rms * gains).astype(jnp.bfloat16)


def project_rows(x_ref, w_refs, rows, gq, gk, put):
    x = x_ref[rows, :]
    for kind in range(3):
        w = [w_ref[kind] for w_ref in w_refs]
        w = w[0] if len(w) == 1 else jnp.concatenate(w, axis=1)
        product = jnp.dot(x, w, preferred_element_type=jnp.float32)
        for j in range(len(w_refs)):
            part = product[:, j * HD : (j + 1) * HD]
            if kind == 0:
                part = normed_head(part, gq)
            elif kind == 1:
                part = normed_head(part, gk)
            else:
                part = part.astype(jnp.bfloat16)
            put(kind, j, part)


def time_project_kernel(pair, heads, x_ref, gq_ref, gk_ref, *refs):
    w_refs, out_ref = refs[:pair], refs[pair]
    frames, _, _, pos, _ = out_ref.shape
    step = chunk_rows(x_ref.shape[0], 512)
    per = step // pos
    gq, gk = gq_ref[...], gk_ref[...]

    def body(m, carry):
        def put(kind, j, value):
            out_ref[pl.ds(m * per, per), kind, j] = value.reshape(per, pos, HD)

        project_rows(x_ref, w_refs, pl.ds(pl.multiple_of(m * step, step), step), gq, gk, put)
        return carry

    lax.fori_loop(0, x_ref.shape[0] // step, body, 0)


def time_project(tokens, weight, gq, gk, heads, frames):
    rows, d = tokens.shape
    count = heads.shape[0]
    pair = 2 if count % 2 == 0 else 1
    pos = rows // frames

    def w_spec(j):
        return pl.BlockSpec((3, d, HD), lambda i, t: (0, 0, t[pair * i + j]))

    gain = pl.BlockSpec((1, HD), lambda i, t: (0, 0))
    return pl.pallas_call(
        functools.partial(time_project_kernel, pair),
        out_shape=jax.ShapeDtypeStruct((frames, 3, count, pos, HD), jnp.bfloat16),
        grid_spec=pltpu.PrefetchScalarGridSpec(
            num_scalar_prefetch=1,
            grid=(count // pair,),
            in_specs=[
                pl.BlockSpec((rows, d), lambda i, t: (0, 0), pipeline_mode=pl.Buffered(1)),
                gain,
                gain,
            ]
            + [w_spec(j) for j in range(pair)],
            out_specs=pl.BlockSpec((frames, 3, pair, pos, HD), lambda i, t: (0, 0, i, 0, 0)),
        ),
        compiler_params=pltpu.CompilerParams(vmem_limit_bytes=VMEM_LIMIT),
        cost_estimate=pl.CostEstimate(
            flops=2 * rows * d * 3 * count * HD,
            bytes_accessed=2 * (rows * d + 3 * d * count * HD + 3 * rows * count * HD),
            transcendentals=0,
        ),
        name="time_project",
    )(heads, tokens, gq, gk, *([weight] * pair))


def space_project_kernel(pair, table, x_ref, gq_ref, gk_ref, after_ref, *refs):
    w_refs, (out_ref, next_ref, prev_ref) = refs[:pair], refs[pair:]
    i = pl.program_id(0)
    count = pl.num_programs(0) * pair
    step = chunk_rows(x_ref.shape[0], 512)
    gq, gk = gq_ref[...], gk_ref[...]

    def body(m, carry):
        rows = pl.ds(pl.multiple_of(m * step, step), step)

        def put(kind, j, value):
            out_ref[kind, j, rows, :] = value

        project_rows(x_ref, w_refs, rows, gq, gk, put)
        return carry

    lax.fori_loop(0, x_ref.shape[0] // step, body, 0)
    for j in range(pair):
        head = i * pair + j
        for s in range(NEAR_MAX):
            for side, ref in ((0, next_ref), (1, prev_ref)):
                b = table[count + (head * 2 + side) * NEAR_MAX + s]
                src = pl.ds(pl.multiple_of(b * BLOCK, BLOCK), BLOCK)
                ref[0, j, s * BLOCK : (s + 1) * BLOCK, :] = out_ref[1, j, src, :]
                ref[1, j, s * BLOCK : (s + 1) * BLOCK, :] = out_ref[2, j, src, :]


def space_project(tokens, weight, gq, gk, heads, picks, after):
    rows, d = tokens.shape
    count = heads.shape[0]
    pair = 2
    near = NEAR_MAX * BLOCK
    table = jnp.concatenate([heads, picks.reshape(-1)])

    def w_spec(j):
        return pl.BlockSpec((3, d, HD), lambda i, t: (0, 0, t[pair * i + j]))

    gain = pl.BlockSpec((1, HD), lambda i, t: (0, 0))
    near_spec = pl.BlockSpec((2, pair, near, HD), lambda i, t: (0, i, 0, 0))
    near_shape = jax.ShapeDtypeStruct((2, count, near, HD), jnp.bfloat16)
    return pl.pallas_call(
        functools.partial(space_project_kernel, pair),
        out_shape=(jax.ShapeDtypeStruct((3, count, rows, HD), jnp.bfloat16), near_shape, near_shape),
        grid_spec=pltpu.PrefetchScalarGridSpec(
            num_scalar_prefetch=1,
            grid=(count // pair,),
            in_specs=[
                pl.BlockSpec((rows, d), lambda i, t: (0, 0), pipeline_mode=pl.Buffered(1)),
                gain,
                gain,
                pl.BlockSpec(memory_space=pl.ANY),
            ]
            + [w_spec(j) for j in range(pair)],
            out_specs=(
                pl.BlockSpec((3, pair, rows, HD), lambda i, t: (0, i, 0, 0)),
                near_spec,
                near_spec,
            ),
        ),
        compiler_params=pltpu.CompilerParams(vmem_limit_bytes=VMEM_LIMIT),
        cost_estimate=pl.CostEstimate(
            flops=2 * rows * d * 3 * count * HD,
            bytes_accessed=2 * (rows * d + 3 * d * count * HD + 3 * rows * count * HD),
            transcendentals=0,
        ),
        name="space_project",
    )(table, tokens, gq, gk, after, *([weight] * pair))


def attend_rows(queries, keys, values, factor):
    scores = lax.dot_general(
        queries, keys, (((1,), (1,)), ((), ())), preferred_element_type=jnp.float32
    )
    weight = jnp.exp2(scores * factor).astype(jnp.bfloat16)
    both = jnp.dot(weight, values, preferred_element_type=jnp.float32)
    return (both[:, :HD] / both[:, HD:]).astype(jnp.bfloat16)


def space_attend_kernel(factor, parts, own_half, qkv_ref, prev_ref, next_ref, bias_ref, out_ref, ka, va, marks):
    rows = qkv_ref.shape[1]
    near = prev_ref.shape[1]
    total = rows + 2 * near

    @pl.when(pl.program_id(0) == 0)
    def _():
        va[:, HD:] = jnp.ones((total, HD), jnp.bfloat16)
        row = lax.broadcasted_iota(jnp.int32, (rows, HD), 0) // BLOCK
        lane = lax.broadcasted_iota(jnp.int32, (rows, HD), 1)
        marks[...] = jnp.where(row == lane, 1.0, 0.0).astype(jnp.bfloat16)

    for slot, ref in ((0, ka), (1, va)):
        ref[:rows, :HD] = qkv_ref[1 + slot]
        ref[rows : rows + near, :HD] = prev_ref[slot]
        ref[rows + near :, :HD] = next_ref[slot]
    for b in range(total // BLOCK):
        ka[b * BLOCK : (b + 1) * BLOCK, HD:] = jnp.broadcast_to(
            bias_ref[b : b + 1, :], (BLOCK, HD)
        ).astype(jnp.bfloat16)
    part = rows // parts
    step = chunk_rows(part, 256)
    for m in range(rows // step):
        span = slice(m * step, (m + 1) * step)
        queries = jnp.concatenate([qkv_ref[0, span, :], marks[span, :]], axis=1)
        result = attend_rows(queries, ka[...], va[...], factor)
        which = lax.rem(m * step // part - own_half[0] + parts, parts)
        first = (m * step) % part
        out_ref[which, first : first + step, :] = result


def space_attend(qkv, prev_kv, next_kv, bias, parts, shift):
    _, count, rows, _ = qkv.shape
    near = prev_kv.shape[2]
    total = rows + 2 * near
    factor = math.log2(math.e) / math.sqrt(HD)
    near_spec = pl.BlockSpec((2, None, near, HD), lambda h, t: (0, h, 0, 0))
    return pl.pallas_call(
        functools.partial(space_attend_kernel, factor, parts),
        out_shape=jax.ShapeDtypeStruct((parts, count, rows // parts, HD), jnp.bfloat16),
        grid_spec=pltpu.PrefetchScalarGridSpec(
            num_scalar_prefetch=1,
            grid=(count,),
            in_specs=[
                pl.BlockSpec((3, None, rows, HD), lambda h, t: (0, h, 0, 0)),
                near_spec,
                near_spec,
                pl.BlockSpec((None, total // BLOCK, HD), lambda h, t: (h, 0, 0)),
            ],
            out_specs=pl.BlockSpec((parts, None, rows // parts, HD), lambda h, t: (0, h, 0, 0)),
            scratch_shapes=[
                pltpu.VMEM((total, 2 * HD), jnp.bfloat16),
                pltpu.VMEM((total, 2 * HD), jnp.bfloat16),
                pltpu.VMEM((rows, HD), jnp.bfloat16),
            ],
        ),
        compiler_params=pltpu.CompilerParams(vmem_limit_bytes=VMEM_LIMIT),
        cost_estimate=pl.CostEstimate(
            flops=8 * count * rows * total * HD,
            bytes_accessed=2 * HD * count * (4 * rows + 4 * near),
            transcendentals=count * rows * total,
        ),
        name="space_attend",
    )(shift, qkv, prev_kv, next_kv, bias)


def time_attend_kernel(factor, blocks, mask, x_ref, out_ref, ka, va):
    frames, _, pos, _ = x_ref.shape
    rows = frames * pos
    span = pos * (BLOCK // STRIP)
    head = pl.program_id(0)
    ka[:, :HD] = x_ref[:, 1].reshape(rows, HD)
    va[:, :HD] = x_ref[:, 2].reshape(rows, HD)
    va[:, HD:] = jnp.ones((rows, HD), jnp.bfloat16)
    row = lax.broadcasted_iota(jnp.int32, (rows, HD), 0)
    lane = lax.broadcasted_iota(jnp.int32, (rows, HD), 1)
    strip = lax.rem(row, pos) // STRIP
    block = row // span
    lane_strip, lane_block = lane // blocks, lax.rem(lane, blocks)
    live = jnp.zeros((rows, HD), jnp.float32)
    for a in range(blocks):
        for b in range(blocks):
            m = mask[(head * blocks + a) * blocks + b].astype(jnp.float32)
            live = jnp.where((lane_block == a) & (block == b), m, live)
    live = jnp.where(strip == lane_strip, live, 0.0)
    ka[:, HD:] = ((live - 1.0) * BIG).astype(jnp.bfloat16)
    marks = jnp.where(strip * blocks + block == lane, 1.0, 0.0).astype(jnp.bfloat16)
    queries = jnp.concatenate([x_ref[:, 0].reshape(rows, HD), marks], axis=1)
    step = chunk_rows(rows, 256)
    per = step // pos
    for m in range(rows // step):
        result = attend_rows(queries[m * step : (m + 1) * step], ka[...], va[...], factor)
        out_ref[m * per : (m + 1) * per] = result.reshape(per, pos, HD)


def time_attend(received, mask):
    frames, _, count, pos, _ = received.shape
    rows = frames * pos
    factor = math.log2(math.e) / math.sqrt(HD)
    return pl.pallas_call(
        functools.partial(time_attend_kernel, factor, mask.shape[1]),
        out_shape=jax.ShapeDtypeStruct((frames, count, pos, HD), jnp.bfloat16),
        grid_spec=pltpu.PrefetchScalarGridSpec(
            num_scalar_prefetch=1,
            grid=(count,),
            in_specs=[pl.BlockSpec((frames, 3, None, pos, HD), lambda h, t: (0, 0, h, 0, 0))],
            out_specs=pl.BlockSpec((frames, None, pos, HD), lambda h, t: (0, h, 0, 0)),
            scratch_shapes=[
                pltpu.VMEM((rows, 2 * HD), jnp.bfloat16),
                pltpu.VMEM((rows, 2 * HD), jnp.bfloat16),
            ],
        ),
        compiler_params=pltpu.CompilerParams(vmem_limit_bytes=VMEM_LIMIT),
        cost_estimate=pl.CostEstimate(
            flops=8 * count * rows * rows * HD,
            bytes_accessed=8 * HD * count * rows,
            transcendentals=count * rows * rows,
        ),
        name="time_attend",
    )(mask.reshape(-1), received)


def assemble_kernel(table, sk_ref, sr_ref, tk_ref, tr_ref, out_ref):
    g = pl.program_id(0)
    groups = pl.num_programs(0)
    slot = table[g]
    other = table[groups + g]
    rows = out_ref.shape[0]

    def write(s_ref, t_ref):
        first, second = s_ref[0], s_ref[1]
        timed = t_ref[...].reshape(rows, HD)
        for want in range(3):

            @pl.when(slot == want)
            def _():
                order = [first, second]
                order.insert(want, timed)
                for c in range(3):
                    out_ref[:, c * HD : (c + 1) * HD] = order[c]

    @pl.when(other == 0)
    def _():
        write(sk_ref, tk_ref)

    @pl.when(other == 1)
    def _():
        write(sr_ref, tr_ref)


def assemble(slots, other, space_at, time_side, group_at, space_keep, space_recv, time_keep, time_recv, chunks):
    groups = slots.shape[0]
    rows = space_keep.shape[1]
    pos = time_keep.shape[2]
    table = jnp.concatenate([slots, other, space_at, time_side, group_at])
    space_spec = pl.BlockSpec((2, rows, HD), lambda g, t: (t[2 * groups + g], 0, 0))
    time_spec = pl.BlockSpec(
        (chunks, None, pos, HD), lambda g, t: (t[3 * groups + g], t[4 * groups + g], 0, 0)
    )
    return pl.pallas_call(
        assemble_kernel,
        out_shape=jax.ShapeDtypeStruct((rows, groups * 3 * HD), jnp.bfloat16),
        grid_spec=pltpu.PrefetchScalarGridSpec(
            num_scalar_prefetch=1,
            grid=(groups,),
            in_specs=[space_spec, space_spec, time_spec, time_spec],
            out_specs=pl.BlockSpec((rows, 3 * HD), lambda g, t: (0, g)),
        ),
        cost_estimate=pl.CostEstimate(
            flops=0, bytes_accessed=8 * rows * groups * 3 * HD, transcendentals=0
        ),
        name="assemble",
    )(table, space_keep, space_recv, time_keep, time_recv)


def block_picks(live):
    used = jnp.max(live, axis=1)
    width = used.shape[1]
    before = (jnp.arange(width)[:, None] < jnp.arange(width)[None, :]).astype(jnp.int32)
    rank = jnp.sum(used[:, :, None] * before[None], axis=1)
    return used[:, None, :] * (rank[:, None, :] == jnp.arange(NEAR_MAX)[None, :, None]).astype(jnp.int32)


def on_device(tokens, qkv_weight, query_gain, key_gain, labels, space_mask, time_mask):
    frame_count = lax.axis_size("frame")
    sides = lax.axis_size("head")
    own_frame = lax.axis_index("frame")
    own_side = lax.axis_index("head")
    row_count = tokens.shape[0]
    groups = labels.shape[0] // 3
    blocks = row_count // BLOCK
    space_count = 2 * groups
    gq, gk = query_gain.reshape(1, HD), key_gain.reshape(1, HD)

    picked = labels.reshape(groups, 3)
    time_slot = jnp.sum(picked * jnp.arange(3, dtype=jnp.int32)[None, :], axis=1)
    group_base = 3 * jnp.arange(groups, dtype=jnp.int32)
    time_heads = group_base + time_slot
    first_space = group_base + jnp.where(time_slot == 0, 1, 0)
    second_space = group_base + jnp.where(time_slot == 2, 1, 2)
    space_heads = jnp.stack([first_space, second_space], axis=1).reshape(space_count)

    packed = time_project(tokens, qkv_weight, gq, gk, time_heads, frame_count)
    received = lax.all_to_all(packed, "frame", split_axis=0, concat_axis=0, tiled=True)

    live = jnp.take(space_mask, space_heads, axis=0)
    low, own, high = live[:, :, :blocks], live[:, :, blocks : 2 * blocks], live[:, :, 2 * blocks :]
    low_pick, high_pick = block_picks(low), block_picks(high)
    ids = jnp.arange(blocks, dtype=jnp.int32)
    picks = jnp.stack([jnp.sum(low_pick * ids, axis=-1), jnp.sum(high_pick * ids, axis=-1)], axis=1)
    low_ok = (own_frame > 0).astype(jnp.int32)
    high_ok = (own_frame < frame_count - 1).astype(jnp.int32)

    def near_live(pick, side, ok):
        return ok * jnp.sum(pick[:, :, None, :] * side[:, None, :, :], axis=-1)

    allowed = jnp.concatenate(
        [jnp.swapaxes(own, 1, 2), near_live(low_pick, low, low_ok), near_live(high_pick, high, high_ok)],
        axis=1,
    )
    bias = jnp.pad((allowed.astype(jnp.float32) - 1.0) * BIG, ((0, 0), (0, 0), (0, HD - blocks)))

    qkv, to_next, to_prev = space_project(tokens, qkv_weight, gq, gk, space_heads, picks, packed)
    up = [(i, i + 1) for i in range(frame_count - 1)]
    down = [(i + 1, i) for i in range(frame_count - 1)]
    prev_kv = lax.ppermute(to_next, "frame", up)
    next_kv = lax.ppermute(to_prev, "frame", down)

    shift = own_side if sides == 2 else jnp.int32(0)
    space_out = space_attend(
        qkv, prev_kv, next_kv, bias, sides, jnp.reshape(shift, (1,)).astype(jnp.int32)
    )
    time_out = time_attend(received, jnp.take(time_mask, time_heads, axis=0))
    returned = lax.all_to_all(time_out, "frame", split_axis=0, concat_axis=0, tiled=True)

    part_rows = row_count // sides
    chunks = frame_count // sides
    side_ids = jnp.repeat(jnp.arange(sides, dtype=jnp.int32), groups)
    group_ids = jnp.tile(jnp.arange(groups, dtype=jnp.int32), sides)
    zeros = jnp.zeros_like(side_ids)
    if sides == 2:
        swap = [(0, 1), (1, 0)]
        their_slot = lax.ppermute(time_slot, "head", swap)
        slots = jnp.where(
            own_side == 0,
            jnp.concatenate([time_slot, their_slot]),
            jnp.concatenate([their_slot, time_slot]),
        )
        space_keep = space_out[0]
        space_recv = lax.ppermute(space_out[1], "head", swap)
        time_keep = lax.dynamic_slice_in_dim(returned, own_side * chunks, chunks, 0)
        time_recv = lax.ppermute(
            lax.dynamic_slice_in_dim(returned, (1 - own_side) * chunks, chunks, 0), "head", swap
        )
        other = (side_ids != own_side).astype(jnp.int32)
        space_at, time_side = group_ids, zeros
    else:
        slots = lax.all_to_all(
            jnp.broadcast_to(time_slot[None], (sides, groups)), "head", 0, 0, tiled=True
        ).reshape(-1)
        space_keep = lax.all_to_all(space_out, "head", 0, 0, tiled=True)
        space_keep = space_keep.reshape(sides * space_count, part_rows, HD)
        space_recv = space_keep
        time_keep = lax.all_to_all(returned, "head", 0, 0, tiled=True)
        time_recv = time_keep
        other, space_at, time_side = zeros, side_ids * groups + group_ids, side_ids
    return assemble(
        slots, other, space_at, time_side, group_ids, space_keep, space_recv, time_keep, time_recv, chunks
    )


def solution(mesh):
    placed = (
        P("frame", None),
        P(None, None, "head"),
        P(),
        P(),
        P("head"),
        P("head", None, None),
        P("head", None, None),
    )
    return jax.shard_map(
        on_device, mesh=mesh, in_specs=placed, out_specs=P(("frame", "head"), None), check_vma=False
    )
```

time: 345 us -> 199 us (0.58)
  matrix products: 90.6 us -> 0 us
  Pallas kernels: 0 us -> 84.4 us
  local copies, waits for them, and re-layouts: 84.5 us -> 11.3 us
  waiting for transfers between devices: 35.6 us -> 75.9 us
  blocking collectives: 38.1 us -> 0 us
  other arithmetic: 40 us -> 4.84 us
  starting transfers between devices: 52.1 us -> 21.6 us
    dot_general x5 -> x0, matrix products: 90.6 us -> none  [the longest x1 37.4 us: on_device(): jnp.einsum('td,kdc->ktc', tokens, qkv_weight, preferred_element_type=jnp....]
    pallas_call x0 -> x5, Pallas kernels: none -> 84.4 us  [the longest x1 28.6 us: space_project(): pl.pallas_call(functools.partial(space_project_kernel, pair), out_shape=(...]
    all_to_all x1 -> x0, blocking collectives: 38.1 us -> none  [on_device(): lax.all_to_all(result, 'head', split_axis=0, concat_axis=1, tiled=True)]
    all_to_all x2, starting transfers between devices: 47.5 us -> 12.6 us  [the longest x1 6.38 us: on_device(): lax.all_to_all(time_out, 'frame', split_axis=0, concat_axis=0, tiled=True)]
    ppermute x2 -> x5, waiting for transfers between devices: 16.3 us -> 47.4 us  [the longest x1 29 us: on_device(): their_slot = lax.ppermute(time_slot, 'head', swap)]
    gather x10 -> x3, local copies, waits for them, and re-layouts: 25.4 us -> 1.23 us  [the longest x2 0.66 us: on_device(): live = jnp.take(space_mask, space_heads, axis=0)]
    slice x4 -> x2, local copies, waits for them, and re-layouts: 19.7 us -> 0.15 us  [the longest x1 0.08 us: on_device(): live[:, :, 2 * blocks:]]
    convert_element_type x3 -> x2, other arithmetic: 10.6 us -> 0.01 us  [the longest x1 0.01 us: block_picks(): (jnp.arange(width)[:, None] < jnp.arange(width)[None, :]).astype(jnp.int32)]
  transfers between devices with their start and end apart: 4 -> 7, of which waited for: 3 -> 3; matrix products, arithmetic and copies ran while one was open for 30% -> 6% of each run, Pallas kernels for 0% -> 30%
where the time goes in v1:
time: 199 us; the launch traced here: 198 us
  Pallas kernels  84.4 us (42%)
  waiting for transfers between devices  75.9 us (38%)
  starting transfers between devices  21.6 us (11%)
  local copies, waits for them, and re-layouts  11.3 us (6%)
  other arithmetic  4.84 us (2%)
    ppermute x1, waiting for transfers between devices, on_device(): their_slot = lax.ppermute(time_slot, 'head', swap)  29 us
    pallas_call x1, Pallas kernels, space_project(): pl.pallas_call(functools.partial(space_project_kernel, pair), out_shape=(...  28.6 us
    all_to_all x1, waiting for transfers between devices, on_device(): lax.all_to_all(packed, 'frame', split_axis=0, concat_axis=0, tiled=True)  28.4 us
    pallas_call x1, Pallas kernels, space_attend(): pl.pallas_call(functools.partial(space_attend_kernel, factor, parts), out...  22.6 us
    ppermute x1, waiting for transfers between devices, on_device(): prev_kv = lax.ppermute(to_next, 'frame', up)  18.4 us
    pallas_call x1, Pallas kernels, time_project(): pl.pallas_call(functools.partial(time_project_kernel, pair), out_shape=ja...  16.9 us
    pallas_call x1, Pallas kernels, time_attend(): pl.pallas_call(functools.partial(time_attend_kernel, factor, mask.shape[1...  8.55 us
    pallas_call x1, Pallas kernels, assemble(): pl.pallas_call(assemble_kernel, out_shape=jax.ShapeDtypeStruct((rows, gro...  7.63 us
  transfers between devices with their start and end apart: 7, of which 3 were waited for; matrix products, arithmetic and copies ran while one was open for 6% of the time, Pallas kernels for 30%

profile of v1, /device:TPU:18, one launch (start us, length us, event | category | flops | bytes accessed | tf_op | source)
XLA Modules:
  0.0 198.1 jit_solution(191227708429837587)
XLA Ops:
  0.0 0.8 reshape.150
  0.8 0.1 multiply_reduce_fusion.6
  0.9 0.6 multiply_add_fusion.heads
  1.5 16.9 %time_project.1.after_ref = bf16[16,3,4,64,128]{4,3,2,1,0:T(8,128)(2,1)} custom-call(s32[4]{0:T(128)} %multiply_add_fusion.heads, bf16[1024,3072]{1,0:T(8,128)(2,1)} %x_ref.3, f32[1,128]{1,0:T(1,128)} %bitcast.23, f32[1,128]{1,0:T(1,128)} %bitcast.25, bf16[3,3072,1536]{2,1,0:T(8,128)(2,1)} %refs_1_.3, bf16[3,3072,1536]{2,1,0:T(8,128)(2,1)} %refs_1_.3), custom_call_target="tpu_custom_call" | custom-call | flops 9663676416 | bytes 18874368 | tf_op jit(solution)/shard_map/time_project/pallas_call | solution.py:75
  18.4 6.2 %all-to-all-start = ((bf16[16,3,4,64,128]{4,3,2,1,0:T(8,128)(2,1)}), bf16[16,3,4,64,128]{4,3,2,1,0:T(8,128)(2,1)S(1)}, u32[]{:S(2)}, u32[]{:S(2)}) async-start(bf16[16,3,4,64,128]{4,3,2,1,0:T(8,128)(2,1)} %time_project.1.after_ref), calls=%async_computation | async-start | bytes 6291456 | tf_op jit(solution)/shard_map/all_to_all | solution.py:380
  24.6 0.1 copy.21
  24.7 0.1 reshape.152
  24.8 0.1 reshape.153
  24.9 0.6 gather_fusion
  25.5 0.1 copy.23
  25.6 0.1 broadcast_select_fusion
  25.7 0.3 slice_reduce_fusion.1
  26.1 0.1 multiply_reduce_fusion.3
  26.2 0.3 fusion.2
  26.6 0.1 reshape.154
  26.7 0.7 pad_add_fusion.2.table
  27.3 28.6 %space_project.1 = (bf16[3,8,1024,128]{3,2,1,0:T(8,128)(2,1)}, bf16[2,8,512,128]{3,2,1,0:T(8,128)(2,1)}, bf16[2,8,512,128]{3,2,1,0:T(8,128)(2,1)}) custom-call(s32[136]{0:T(256)} %pad_add_fusion.2.table, bf16[1024,3072]{1,0:T(8,128)(2,1)} %x_ref.3, f32[1,128]{1,0:T(1,128)} %bitcast.24, f32[1,128]{1,0:T(1,128)} %bitcast.26, ...), custom_call_target="tpu_custom_call" | custom-call | flops 19327352832 | bytes 31457280 | tf_op jit(solution)/shard_map/space_project/pallas_call | solution.py:139
  56.0 2.0 %collective-permute-start.1 = (bf16[2,8,512,128]{3,2,1,0:T(8,128)(2,1)}, bf16[2,8,512,128]{3,2,1,0:T(8,128)(2,1)}, u32[]{:S(2)}, u32[]{:S(2)}) collective-permute-start(bf16[2,8,512,128]{3,2,1,0:T(8,128)(2,1)} %get-tuple-element.9), channel_id=1, source_target_pairs={{0,2},{2,4},{4,6},{6,8},{8,10},{10,12},{12,14},{14,16},{16,18},{18... | collective-permute-start | bytes 6291464 | tf_op jit(solution)/shard_map/ppermute | solution.py:402
  58.0 4.4 %collective-permute-start.2 = (bf16[2,8,512,128]{3,2,1,0:T(8,128)(2,1)}, bf16[2,8,512,128]{3,2,1,0:T(8,128)(2,1)}, u32[]{:S(2)}, u32[]{:S(2)}) collective-permute-start(bf16[2,8,512,128]{3,2,1,0:T(8,128)(2,1)} %get-tuple-element.10), channel_id=1, source_target_pairs={{2,0},{4,2},{6,4},{8,6},{10,8},{12,10},{14,12},{16,14},{18,16},{20... | collective-permute-start | bytes 6291464 | tf_op jit(solution)/shard_map/ppermute | solution.py:403
  62.4 0.1 copy.27
  62.6 0.6 gather_fusion.1
  63.1 0.1 broadcast_select_fusion.1
  63.2 0.6 select_n.89.mask
  63.8 0.1 copy.25
  63.9 0.1 copy.26
  64.0 1.2 multiply_reduce_fusion.1
  65.2 1.2 multiply_reduce_fusion
  66.4 0.7 pad.4.bias_ref
  67.0 28.4 %all-to-all-done.x_ref = bf16[16,3,4,64,128]{4,3,2,1,0:T(8,128)(2,1)S(1)} async-done(((bf16[16,3,4,64,128]{4,3,2,1,0:T(8,128)(2,1)}), bf16[16,3,4,64,128]{4,3,2,1,0:T(8,128)(2,1)S(1)}, u32[]{:S(2)}, u32[]{:S(2)}) %all-to-all-start) | async-done | bytes 3145760 | tf_op jit(solution)/shard_map/all_to_all | solution.py:380
  95.5 1.7 copy-done.2
  97.1 8.5 %time_attend.1 = bf16[16,4,64,128]{3,2,1,0:T(8,128)(2,1)} custom-call(s32[16]{0:T(128)} %select_n.89.mask, bf16[16,3,4,64,128]{4,3,2,1,0:T(8,128)(2,1)} %copy-done.2), custom_call_target="tpu_custom_call" | custom-call | flops 4294967296 | bytes 4194304 | tf_op jit(solution)/shard_map/time_attend/pallas_call | solution.py:276
  105.7 6.4 %all-to-all-start.1 = ((bf16[16,4,64,128]{3,2,1,0:T(8,128)(2,1)}), bf16[16,4,64,128]{3,2,1,0:T(8,128)(2,1)S(1)}, u32[]{:S(2)}, u32[]{:S(2)}) async-start(bf16[16,4,64,128]{3,2,1,0:T(8,128)(2,1)} %time_attend.1), calls=%async_computation.1 | async-start | bytes 2097152 | tf_op jit(solution)/shard_map/all_to_all | solution.py:410
  112.1 18.4 %collective-permute-done.1.prev_ref = bf16[2,8,512,128]{3,2,1,0:T(8,128)(2,1)} collective-permute-done((bf16[2,8,512,128]{3,2,1,0:T(8,128)(2,1)}, bf16[2,8,512,128]{3,2,1,0:T(8,128)(2,1)}, u32[]{:S(2)}, u32[]{:S(2)}) %collective-permute-start.1) | collective-permute-done | bytes 2097184 | tf_op jit(solution)/shard_map/ppermute | solution.py:402
  130.5 22.6 %space_attend.1 = bf16[2,8,512,128]{3,2,1,0:T(8,128)(2,1)} custom-call(s32[1]{0:T(128)} %bitcast.own_half, bf16[3,8,1024,128]{3,2,1,0:T(8,128)(2,1)} %get-tuple-element.8.qkv_ref, bf16[2,8,512,128]{3,2,1,0:T(8,128)(2,1)} %collective-permute-done.1.prev_ref, bf16[2,8,512,128]{3,2,1,0:T(8,128)(2,1)} %collective-permute-done.2.next_ref, f32[8,32,128]{2,1,0:T(8,128)} %pad.4.bias_ref), custom_call_target="tpu_custom_call" | custom-call | flops 17179869184 | bytes 12582912 | tf_op jit(solution)/shard_map/space_attend/pallas_call | solution.py:214
  153.1 2.7 %slice_bitcast_fusion = (bf16[8,512,128]{2,1,0:T(8,128)(2,1)S(1)}, bf16[8,512,128]{2,1,0:T(8,128)(2,1)}) fusion(bf16[2,8,512,128]{3,2,1,0:T(8,128)(2,1)} %space_attend.1), kind=kLoop, calls=%fused_computation.2 | loop fusion | bytes 4194304 | tf_op jit(solution)/shard_map/squeeze | solution.py:426
  155.8 0.6 collective-permute-start.3
  156.4 1.1 constant_dynamic-slice_fusion
  157.4 1.5 collective-permute-start.4
  158.9 0.6 collective-permute-start
  159.5 0.1 reshape.157
  159.6 0.1 tile.14
  159.6 29.0 %collective-permute-done = s32[4]{0:T(128)S(1)} collective-permute-done((s32[4]{0:T(128)S(1)}, s32[4]{0:T(128)S(1)}, u32[]{:S(2)}, u32[]{:S(2)}) %collective-permute-start) | collective-permute-done | bytes 48 | tf_op jit(solution)/shard_map/ppermute | solution.py:419
  188.7 0.1 broadcast_select_fusion.2
  188.7 0.6 concatenate.17.table
  189.3 0.0 copy-start.1
  189.3 1.0 copy-done.3
  190.3 0.2 copy-done.4
  190.5 7.6 %assemble.1 = bf16[512,3072]{1,0:T(8,128)(2,1)} custom-call(s32[40]{0:T(128)} %concatenate.17.table, bf16[8,512,128]{2,1,0:T(8,128)(2,1)} %get-tuple-element.16.sk_ref, bf16[8,512,128]{2,1,0:T(8,128)(2,1)} %copy-done.3, bf16[8,4,64,128]{3,2,1,0:T(8,128)(2,1)} %get-tuple-element.18.tk_ref, bf16[8,4,64,128]{3,2,1,0:T(8,128)(2,1)} %copy-done.4), custom_call_target="tpu_custom_call" | custom-call | bytes 12582912 | tf_op jit(solution)/shard_map/assemble/pallas_call | solution.py:336
  (28 shorter events, 0.1 us)
Async XLA Ops:
  0.0 24.9 %copy-start = (s32[12,16,48]{2,1,0:T(8,128)S(1)}, s32[12,16,48]{2,1,0:T(8,128)}, u32[]{:S(2)}) copy-start(s32[12,16,48]{2,1,0:T(8,128)} %param.12) | copy-start | bytes 110596
  18.4 77.0 %all-to-all-start = ((bf16[16,3,4,64,128]{4,3,2,1,0:T(8,128)(2,1)}), bf16[16,3,4,64,128]{4,3,2,1,0:T(8,128)(2,1)S(1)}, u32[]{:S(2)}, u32[]{:S(2)}) async-start(bf16[16,3,4,64,128]{4,3,2,1,0:T(8,128)(2,1)} %time_project.1.after_ref), calls=%async_computation | async-start | bytes 6291456 | tf_op jit(solution)/shard_map/all_to_all | solution.py:380
  27.3 35.1 %copy-start.5 = (s32[12,2,2]{0,2,1:T(2,128)S(1)}, s32[12,2,2]{0,2,1:T(2,128)}, u32[]{:S(2)}) copy-start(s32[12,2,2]{0,2,1:T(2,128)} %param.13) | copy-start | bytes 580
  56.0 74.5 %collective-permute-start.1 = (bf16[2,8,512,128]{3,2,1,0:T(8,128)(2,1)}, bf16[2,8,512,128]{3,2,1,0:T(8,128)(2,1)}, u32[]{:S(2)}, u32[]{:S(2)}) collective-permute-start(bf16[2,8,512,128]{3,2,1,0:T(8,128)(2,1)} %get-tuple-element.9), channel_id=1, source_target_pairs={{0,2},{2,4},{4,6},{6,8},{8,10},{10,12},{12,14},{14,16},{16,18},{18... | collective-permute-start | bytes 6291464 | tf_op jit(solution)/shard_map/ppermute | solution.py:402
  58.0 72.5 %collective-permute-start.2 = (bf16[2,8,512,128]{3,2,1,0:T(8,128)(2,1)}, bf16[2,8,512,128]{3,2,1,0:T(8,128)(2,1)}, u32[]{:S(2)}, u32[]{:S(2)}) collective-permute-start(bf16[2,8,512,128]{3,2,1,0:T(8,128)(2,1)} %get-tuple-element.10), channel_id=1, source_target_pairs={{2,0},{4,2},{6,4},{8,6},{10,8},{12,10},{14,12},{16,14},{18,16},{20... | collective-permute-start | bytes 6291464 | tf_op jit(solution)/shard_map/ppermute | solution.py:403
  95.5 1.7 copy-start.2
  105.7 50.7 %all-to-all-start.1 = ((bf16[16,4,64,128]{3,2,1,0:T(8,128)(2,1)}), bf16[16,4,64,128]{3,2,1,0:T(8,128)(2,1)S(1)}, u32[]{:S(2)}, u32[]{:S(2)}) async-start(bf16[16,4,64,128]{3,2,1,0:T(8,128)(2,1)} %time_attend.1), calls=%async_computation.1 | async-start | bytes 2097152 | tf_op jit(solution)/shard_map/all_to_all | solution.py:410
  155.8 33.5 %collective-permute-start.3 = (bf16[8,512,128]{2,1,0:T(8,128)(2,1)S(1)}, bf16[8,512,128]{2,1,0:T(8,128)(2,1)S(1)}, u32[]{:S(2)}, u32[]{:S(2)}) collective-permute-start(bf16[8,512,128]{2,1,0:T(8,128)(2,1)S(1)} %get-tuple-element.15), channel_id=1, source_target_pairs={{0,1},{1,0},{2,3},{3,2},{4,5},{5,4},{6,7},{7,6},{8,9},{9,8},{10,11... | collective-permute-start | bytes 3145736 | tf_op jit(solution)/shard_map/ppermute | solution.py:426
  157.4 31.9 %collective-permute-start.4 = (bf16[8,4,64,128]{3,2,1,0:T(8,128)(2,1)}, bf16[8,4,64,128]{3,2,1,0:T(8,128)(2,1)S(1)}, u32[]{:S(2)}, u32[]{:S(2)}) collective-permute-start(bf16[8,4,64,128]{3,2,1,0:T(8,128)(2,1)} %get-tuple-element.17), channel_id=1, source_target_pairs={{0,1},{1,0},{2,3},{3,2},{4,5},{5,4},{6,7},{7,6},{8,9},{9,8},{10,11... | collective-permute-start | bytes 1572872 | tf_op jit(solution)/shard_map/ppermute | solution.py:428
  158.9 29.7 %collective-permute-start = (s32[4]{0:T(128)S(1)}, s32[4]{0:T(128)S(1)}, u32[]{:S(2)}, u32[]{:S(2)}) collective-permute-start(s32[4]{0:T(128)S(1)} %multiply_reduce_fusion.6), channel_id=1, source_target_pairs={{0,1},{1,0},{2,3},{3,2},{4,5},{5,4},{6,7},{7,6},{8,9},{9,8},{10,11... | collective-permute-start | bytes 56 | tf_op jit(solution)/shard_map/ppermute | solution.py:419
  189.3 1.0 copy-start.3
  189.3 1.2 copy-start.4
  189.3 8.8 %copy-start.1 = (s32[12,16,48]{2,1,0:T(8,128)S(1)}, s32[12,16,48]{2,1,0:T(8,128)}, u32[]{:S(2)}) copy-start(s32[12,16,48]{2,1,0:T(8,128)} %param.12) | copy-start | bytes 110596

commit v2 on v1

v2 whole, which is shorter than its diff:
```python
import functools
import math

import jax
import jax.numpy as jnp
from jax import lax
from jax.experimental import pallas as pl
from jax.experimental.pallas import tpu as pltpu
from jax.sharding import PartitionSpec as P


STRIP = 8
BLOCK = 64
NEAR_MAX = 8
HD = 128
epsilon = 1e-06
BIG = 1e30
VMEM_LIMIT = 56 * 1024 * 1024


def chunk_rows(rows, want):
    while rows % want:
        want //= 2
    return want


def normed_head(projected, gains):
    inverse_rms = lax.rsqrt(jnp.mean(projected * projected, axis=-1, keepdims=True) + epsilon)
    return (projected * inverse_rms * gains).astype(jnp.bfloat16)


def project_kernel(kinds, pair, near_count, strips, table, x_ref, gq_ref, gk_ref, after_ref, *refs):
    weights = refs[: len(kinds) * pair]
    outs = refs[len(kinds) * pair :]
    out_ref = outs[0]
    i = pl.program_id(0)
    count = pl.num_programs(0) * pair
    step = chunk_rows(x_ref.shape[0], 512)
    gains = {0: gq_ref[...], 1: gk_ref[...]}

    def body(m, carry):
        rows = pl.ds(pl.multiple_of(m * step, step), step)
        x = x_ref[rows, :]
        for n, kind in enumerate(kinds):
            w = [w_ref[...] for w_ref in weights[n * pair : (n + 1) * pair]]
            w = w[0] if pair == 1 else jnp.concatenate(w, axis=1)
            product = jnp.dot(x, w, preferred_element_type=jnp.float32)
            for j in range(pair):
                part = product[:, j * HD : (j + 1) * HD]
                if kind in gains:
                    part = normed_head(part, gains[kind])
                else:
                    part = part.astype(jnp.bfloat16)
                if strips:
                    pos = out_ref.shape[3]
                    per = step // pos
                    out_ref[pl.ds(m * per, per), n, j] = part.reshape(per, pos, HD)
                else:
                    out_ref[n, j, rows, :] = part
        return carry

    lax.fori_loop(0, x_ref.shape[0] // step, body, 0)
    for j in range(pair if near_count else 0):
        head = i * pair + j
        for s in range(near_count):
            for side, ref in ((0, outs[1]), (1, outs[2])):
                b = table[count + (head * 2 + side) * near_count + s]
                src = pl.ds(pl.multiple_of(b * BLOCK, BLOCK), BLOCK)
                for n in range(2):
                    ref[n, j, s * BLOCK : (s + 1) * BLOCK, :] = out_ref[n, j, src, :]


def project(tokens, weight, gq, gk, heads, kinds, after, strips=0, picks=None):
    rows, d = tokens.shape
    count = heads.shape[0]
    pair = 2 if count % 2 == 0 else 1
    n = len(kinds)
    near_count = 0 if picks is None else NEAR_MAX
    table = heads if picks is None else jnp.concatenate([heads, picks.reshape(-1)])

    def w_spec(kind, j):
        return pl.BlockSpec((None, d, HD), lambda i, t: (kind, 0, t[pair * i + j]))

    gain = pl.BlockSpec((1, HD), lambda i, t: (0, 0))
    if strips:
        pos = rows // strips
        shapes = [jax.ShapeDtypeStruct((strips, n, count, pos, HD), jnp.bfloat16)]
        specs = [pl.BlockSpec((strips, n, pair, pos, HD), lambda i, t: (0, 0, i, 0, 0))]
    else:
        shapes = [jax.ShapeDtypeStruct((n, count, rows, HD), jnp.bfloat16)]
        specs = [pl.BlockSpec((n, pair, rows, HD), lambda i, t: (0, i, 0, 0))]
    if near_count:
        near = near_count * BLOCK
        shapes += [jax.ShapeDtypeStruct((2, count, near, HD), jnp.bfloat16)] * 2
        specs += [pl.BlockSpec((2, pair, near, HD), lambda i, t: (0, i, 0, 0))] * 2
    out = pl.pallas_call(
        functools.partial(project_kernel, kinds, pair, near_count, bool(strips)),
        out_shape=tuple(shapes),
        grid_spec=pltpu.PrefetchScalarGridSpec(
            num_scalar_prefetch=1,
            grid=(count // pair,),
            in_specs=[
                pl.BlockSpec((rows, d), lambda i, t: (0, 0), pipeline_mode=pl.Buffered(1)),
                gain,
                gain,
                pl.BlockSpec(memory_space=pl.ANY),
            ]
            + [w_spec(kind, j) for kind in kinds for j in range(pair)],
            out_specs=tuple(specs),
        ),
        compiler_params=pltpu.CompilerParams(vmem_limit_bytes=VMEM_LIMIT),
        cost_estimate=pl.CostEstimate(
            flops=2 * rows * d * n * count * HD,
            bytes_accessed=2 * (rows * d + n * d * count * HD + n * rows * count * HD),
            transcendentals=0,
        ),
    )(table, tokens, gq, gk, after, *([weight] * (n * pair)))
    return out if near_count else out[0]


def attend_rows(queries, keys, values, factor):
    scores = lax.dot_general(
        queries, keys, (((1,), (1,)), ((), ())), preferred_element_type=jnp.float32
    )
    weight = jnp.exp2(scores * factor).astype(jnp.bfloat16)
    both = jnp.dot(weight, values, preferred_element_type=jnp.float32)
    return (both[:, :HD] / both[:, HD:]).astype(jnp.bfloat16)


def space_attend_kernel(factor, parts, side, q_ref, kv_ref, prev_ref, next_ref, bias_ref, after_ref, *refs):
    outs, (ka, va, marks) = refs[:-3], refs[-3:]
    rows = q_ref.shape[0]
    near = prev_ref.shape[1]
    total = rows + 2 * near

    @pl.when(pl.program_id(0) == 0)
    def _():
        va[:, HD:] = jnp.ones((total, HD), jnp.bfloat16)
        row = lax.broadcasted_iota(jnp.int32, (rows, HD), 0) // BLOCK
        lane = lax.broadcasted_iota(jnp.int32, (rows, HD), 1)
        marks[...] = jnp.where(row == lane, 1.0, 0.0).astype(jnp.bfloat16)

    for slot, ref in ((0, ka), (1, va)):
        ref[:rows, :HD] = kv_ref[slot]
        ref[rows : rows + near, :HD] = prev_ref[slot]
        ref[rows + near :, :HD] = next_ref[slot]
    for b in range(total // BLOCK):
        ka[b * BLOCK : (b + 1) * BLOCK, HD:] = jnp.broadcast_to(
            bias_ref[b : b + 1, :], (BLOCK, HD)
        ).astype(jnp.bfloat16)
    part = rows // parts
    step = chunk_rows(part, 256)
    for m in range(rows // step):
        span = slice(m * step, (m + 1) * step)
        queries = jnp.concatenate([q_ref[span, :], marks[span, :]], axis=1)
        result = attend_rows(queries, ka[...], va[...], factor)
        half = m * step // part
        rest = slice(m * step % part, m * step % part + step)
        if len(outs) == 1:
            outs[0][half, rest, :] = result
        else:

            @pl.when(side[0] == half)
            def _():
                outs[0][rest, :] = result

            @pl.when(side[0] != half)
            def _():
                outs[1][rest, :] = result


def space_attend(q, kv, prev_kv, next_kv, bias, first, count, parts, side, after):
    rows = q.shape[2]
    near = prev_kv.shape[2]
    total = rows + 2 * near
    factor = math.log2(math.e) / math.sqrt(HD)
    near_spec = pl.BlockSpec((2, None, near, HD), lambda h, t: (0, first + h, 0, 0))
    part = rows // parts
    if parts == 2:
        shapes = [jax.ShapeDtypeStruct((count, part, HD), jnp.bfloat16)] * 2
        specs = [pl.BlockSpec((None, part, HD), lambda h, t: (h, 0, 0))] * 2
    else:
        shapes = [jax.ShapeDtypeStruct((parts, count, part, HD), jnp.bfloat16)]
        specs = [pl.BlockSpec((parts, None, part, HD), lambda h, t: (0, h, 0, 0))]
    return pl.pallas_call(
        functools.partial(space_attend_kernel, factor, parts),
        out_shape=tuple(shapes),
        grid_spec=pltpu.PrefetchScalarGridSpec(
            num_scalar_prefetch=1,
            grid=(count,),
            in_specs=[
                pl.BlockSpec((None, None, rows, HD), lambda h, t: (0, first + h, 0, 0)),
                pl.BlockSpec((2, None, rows, HD), lambda h, t: (0, first + h, 0, 0)),
                near_spec,
                near_spec,
                pl.BlockSpec((None, total // BLOCK, HD), lambda h, t: (first + h, 0, 0)),
                pl.BlockSpec(memory_space=pl.ANY),
            ],
            out_specs=tuple(specs),
            scratch_shapes=[
                pltpu.VMEM((total, 2 * HD), jnp.bfloat16),
                pltpu.VMEM((total, 2 * HD), jnp.bfloat16),
                pltpu.VMEM((rows, HD), jnp.bfloat16),
            ],
        ),
        compiler_params=pltpu.CompilerParams(vmem_limit_bytes=VMEM_LIMIT),
        cost_estimate=pl.CostEstimate(
            flops=8 * count * rows * total * HD,
            bytes_accessed=2 * HD * count * (4 * rows + 4 * near),
            transcendentals=count * rows * total,
        ),
    )(side, q, kv, prev_kv, next_kv, bias, after)


def time_attend_kernel(factor, blocks, mask, x_ref, after_ref, out_ref, ka, va):
    frames, _, pos, _ = x_ref.shape
    rows = frames * pos
    span = pos * (BLOCK // STRIP)
    head = pl.program_id(0)
    ka[:, :HD] = x_ref[:, 1].reshape(rows, HD)
    va[:, :HD] = x_ref[:, 2].reshape(rows, HD)
    va[:, HD:] = jnp.ones((rows, HD), jnp.bfloat16)
    row = lax.broadcasted_iota(jnp.int32, (rows, HD), 0)
    lane = lax.broadcasted_iota(jnp.int32, (rows, HD), 1)
    strip = lax.rem(row, pos) // STRIP
    block = row // span
    lane_strip, lane_block = lane // blocks, lax.rem(lane, blocks)
    live = jnp.zeros((rows, HD), jnp.float32)
    for a in range(blocks):
        for b in range(blocks):
            m = mask[(head * blocks + a) * blocks + b].astype(jnp.float32)
            live = jnp.where((lane_block == a) & (block == b), m, live)
    live = jnp.where(strip == lane_strip, live, 0.0)
    ka[:, HD:] = ((live - 1.0) * BIG).astype(jnp.bfloat16)
    marks = jnp.where(strip * blocks + block == lane, 1.0, 0.0).astype(jnp.bfloat16)
    queries = jnp.concatenate([x_ref[:, 0].reshape(rows, HD), marks], axis=1)
    step = chunk_rows(rows, 256)
    per = step // pos
    for m in range(rows // step):
        result = attend_rows(queries[m * step : (m + 1) * step], ka[...], va[...], factor)
        out_ref[m * per : (m + 1) * per] = result.reshape(per, pos, HD)


def time_attend(received, mask, after):
    frames, _, count, pos, _ = received.shape
    rows = frames * pos
    factor = math.log2(math.e) / math.sqrt(HD)
    return pl.pallas_call(
        functools.partial(time_attend_kernel, factor, mask.shape[1]),
        out_shape=jax.ShapeDtypeStruct((frames, count, pos, HD), jnp.bfloat16),
        grid_spec=pltpu.PrefetchScalarGridSpec(
            num_scalar_prefetch=1,
            grid=(count,),
            in_specs=[
                pl.BlockSpec((frames, 3, None, pos, HD), lambda h, t: (0, 0, h, 0, 0)),
                pl.BlockSpec(memory_space=pl.ANY),
            ],
            out_specs=pl.BlockSpec((frames, None, pos, HD), lambda h, t: (0, h, 0, 0)),
            scratch_shapes=[
                pltpu.VMEM((rows, 2 * HD), jnp.bfloat16),
                pltpu.VMEM((rows, 2 * HD), jnp.bfloat16),
            ],
        ),
        compiler_params=pltpu.CompilerParams(vmem_limit_bytes=VMEM_LIMIT),
        cost_estimate=pl.CostEstimate(
            flops=8 * count * rows * rows * HD,
            bytes_accessed=8 * HD * count * rows,
            transcendentals=count * rows * rows,
        ),
        name="time_attend",
    )(mask.reshape(-1), received, after)


def assemble_kernel(sources, table, *refs):
    g = pl.program_id(0)
    groups = pl.num_programs(0)
    out_ref = refs[-1]
    slot, chosen = table[g], table[groups + g]
    rows = out_ref.shape[0]
    for n in range(sources):
        s_ref, t_ref = refs[2 * n], refs[2 * n + 1]
        for want in range(3):

            @pl.when((chosen == n) & (slot == want))
            def _():
                order = [s_ref[0], s_ref[1]]
                order.insert(want, t_ref[...].reshape(rows, HD))
                for c in range(3):
                    out_ref[:, c * HD : (c + 1) * HD] = order[c]


def assemble(slots, chosen, sources, chunks):
    groups = slots.shape[0]
    rows = sources[0][0].shape[1]
    tables, specs, arrays = [slots, chosen], [], []
    for n, (space, timed, side, at) in enumerate(sources):
        per = timed.shape[1]
        pos = timed.shape[2]
        tables += [side, at]

        def space_index(g, t, n=n, per=per):
            return (t[(2 + 2 * n) * groups + g] * per + t[(3 + 2 * n) * groups + g], 0, 0)

        def time_index(g, t, n=n):
            return (t[(2 + 2 * n) * groups + g], t[(3 + 2 * n) * groups + g], 0, 0)

        specs += [pl.BlockSpec((2, rows, HD), space_index), pl.BlockSpec((chunks, None, pos, HD), time_index)]
        arrays += [space, timed]
    return pl.pallas_call(
        functools.partial(assemble_kernel, len(sources)),
        out_shape=jax.ShapeDtypeStruct((rows, groups * 3 * HD), jnp.bfloat16),
        grid_spec=pltpu.PrefetchScalarGridSpec(
            num_scalar_prefetch=1,
            grid=(groups,),
            in_specs=specs,
            out_specs=pl.BlockSpec((rows, 3 * HD), lambda g, t: (0, g)),
        ),
        cost_estimate=pl.CostEstimate(
            flops=0, bytes_accessed=4 * rows * groups * 3 * HD, transcendentals=0
        ),
        name="assemble",
    )(jnp.concatenate(tables), *arrays)


def block_picks(live):
    used = jnp.max(live, axis=1)
    width = used.shape[1]
    before = (jnp.arange(width)[:, None] < jnp.arange(width)[None, :]).astype(jnp.int32)
    rank = jnp.sum(used[:, :, None] * before[None], axis=1)
    return used[:, None, :] * (rank[:, None, :] == jnp.arange(NEAR_MAX)[None, :, None]).astype(jnp.int32)


def on_device(tokens, qkv_weight, query_gain, key_gain, labels, space_mask, time_mask):
    frame_count = lax.axis_size("frame")
    sides = lax.axis_size("head")
    own_frame = lax.axis_index("frame")
    own_side = lax.axis_index("head")
    row_count = tokens.shape[0]
    groups = labels.shape[0] // 3
    blocks = row_count // BLOCK
    space_count = 2 * groups
    gq, gk = query_gain.reshape(1, HD), key_gain.reshape(1, HD)

    picked = labels.reshape(groups, 3)
    time_slot = jnp.sum(picked * jnp.arange(3, dtype=jnp.int32)[None, :], axis=1)
    group_base = 3 * jnp.arange(groups, dtype=jnp.int32)
    time_heads = group_base + time_slot
    first_space = group_base + jnp.where(time_slot == 0, 1, 0)
    second_space = group_base + jnp.where(time_slot == 2, 1, 2)
    space_heads = jnp.stack([first_space, second_space], axis=1).reshape(space_count)

    live = jnp.take(space_mask, space_heads, axis=0)
    low, own, high = live[:, :, :blocks], live[:, :, blocks : 2 * blocks], live[:, :, 2 * blocks :]
    low_pick, high_pick = block_picks(low), block_picks(high)
    ids = jnp.arange(blocks, dtype=jnp.int32)
    picks = jnp.stack([jnp.sum(low_pick * ids, axis=-1), jnp.sum(high_pick * ids, axis=-1)], axis=1)
    low_ok = (own_frame > 0).astype(jnp.int32)
    high_ok = (own_frame < frame_count - 1).astype(jnp.int32)

    def near_live(pick, side, ok):
        return ok * jnp.sum(pick[:, :, None, :] * side[:, None, :, :], axis=-1)

    allowed = jnp.concatenate(
        [jnp.swapaxes(own, 1, 2), near_live(low_pick, low, low_ok), near_live(high_pick, high, high_ok)],
        axis=1,
    )
    bias = jnp.pad((allowed.astype(jnp.float32) - 1.0) * BIG, ((0, 0), (0, 0), (0, HD - blocks)))

    swap = [(0, 1), (1, 0)]
    if sides == 2:
        their_slot = lax.ppermute(time_slot, "head", swap)
        picks, their_slot = lax.optimization_barrier((picks, their_slot))

    splits = 2 if groups % 2 == 0 else 1
    share = groups // splits
    up = [(i, i + 1) for i in range(frame_count - 1)]
    down = [(i + 1, i) for i in range(frame_count - 1)]
    received = []
    after = gq
    for n in range(splits):
        packed = project(
            tokens, qkv_weight, gq, gk, time_heads[n * share : (n + 1) * share], (0, 1, 2), after,
            strips=frame_count,
        )
        received.append(lax.all_to_all(packed, "frame", split_axis=0, concat_axis=0, tiled=True))
        after = packed
        if n == 0:
            kv, to_next, to_prev = project(
                tokens, qkv_weight, gq, gk, space_heads, (1, 2), after, picks=picks
            )
            prev_kv = lax.ppermute(to_next, "frame", up)
            next_kv = lax.ppermute(to_prev, "frame", down)
            after = kv
    space_q = project(tokens, qkv_weight, gq, gk, space_heads, (0,), after)

    mask = jnp.take(time_mask, time_heads, axis=0)
    side = jnp.reshape(own_side, (1,)).astype(jnp.int32)
    part_rows = row_count // sides
    chunks = frame_count // sides
    after = space_q
    returned, space_out = [], []

    def timed(n, after):
        out = time_attend(received[n], mask[n * share : (n + 1) * share], after)
        returned.append(lax.all_to_all(out, "frame", split_axis=0, concat_axis=0, tiled=True))
        return out

    if splits == 2:
        after = timed(0, after)
    for n in range(splits):
        out = space_attend(
            space_q, kv, prev_kv, next_kv, bias, n * 2 * share, 2 * share, sides, side, after
        )
        space_out.append(out)
        after = out[0]
    timed(splits - 1, after)

    side_ids = jnp.repeat(jnp.arange(sides, dtype=jnp.int32), groups)
    group_ids = jnp.tile(jnp.arange(groups, dtype=jnp.int32), sides)
    all_ids = jnp.arange(sides * groups, dtype=jnp.int32)
    zeros = jnp.zeros_like(side_ids)
    sources = []
    if sides == 2:
        slots = jnp.where(
            own_side == 0,
            jnp.concatenate([time_slot, their_slot]),
            jnp.concatenate([their_slot, time_slot]),
        )
        for n in range(splits):
            keep, send = space_out[n]
            recv = lax.ppermute(send, "head", swap)
            time_keep = lax.dynamic_slice_in_dim(returned[n], own_side * chunks, chunks, 0)
            time_send = lax.dynamic_slice_in_dim(returned[n], (1 - own_side) * chunks, chunks, 0)
            time_recv = lax.ppermute(time_send, "head", swap)
            for whose, space_part, time_part in ((own_side, keep, time_keep), (1 - own_side, recv, time_recv)):
                at = jnp.clip(all_ids - whose * groups - n * share, 0, share - 1)
                sources.append((space_part, time_part, zeros, at))
        chosen = group_ids // share * 2 + (side_ids != own_side).astype(jnp.int32)
    else:
        slots = lax.all_to_all(
            jnp.broadcast_to(time_slot[None], (sides, groups)), "head", 0, 0, tiled=True
        ).reshape(-1)
        for n in range(splits):
            space_part = lax.all_to_all(space_out[n][0], "head", 0, 0, tiled=True)
            time_part = lax.all_to_all(returned[n], "head", 0, 0, tiled=True)
            at = jnp.clip(group_ids - n * share, 0, share - 1)
            sources.append((space_part.reshape(-1, part_rows, HD), time_part, side_ids, at))
        chosen = group_ids // share
    return assemble(slots, chosen, sources, chunks)


def solution(mesh):
    placed = (
        P("frame", None),
        P(None, None, "head"),
        P(),
        P(),
        P("head"),
        P("head", None, None),
        P("head", None, None),
    )

    return jax.shard_map(
        on_device, mesh=mesh, in_specs=placed, out_specs=P(("frame", "head"), None), check_vma=False
    )
```

time: 199 us -> 211 us (1.060); the launches traced: 198 us -> 208 us
  waiting for transfers between devices: 75.9 us -> 40.4 us
  Pallas kernels: 84.4 us -> 109 us
  starting transfers between devices: 21.6 us -> 44.5 us
  local copies, waits for them, and re-layouts: 11.3 us -> 8.27 us
    ppermute x1, waiting for transfers between devices: 29 us -> 0.01 us  [on_device(): their_slot = lax.ppermute(time_slot, 'head', swap)]
    all_to_all x1 -> x2, waiting for transfers between devices: 28.4 us -> 0.01 us  [on_device(): lax.all_to_all(packed, 'frame', split_axis=0, concat_axis=0, tiled=True)]
    ppermute x2 -> x4, waiting for transfers between devices: 0.01 us -> 20 us  [the longest x2 10.4 us: on_device(): time_recv = lax.ppermute(time_send, 'head', swap)]
    all_to_all x1 -> x2, starting transfers between devices: 6.38 us -> 21.1 us  [timed(): lax.all_to_all(out, 'frame', split_axis=0, concat_axis=0, tiled=True)]
    pallas_call x3 -> x5, Pallas kernels: 53.2 us -> 65.3 us  [the longest x4 57.9 us: project(): pl.pallas_call(functools.partial(project_kernel, kinds, pair, near_count,...]
    pallas_call x1 -> x2, Pallas kernels: 22.6 us -> 32.3 us  [space_attend(): pl.pallas_call(functools.partial(space_attend_kernel, factor, parts), out...]
    all_to_all x1 -> x2, waiting for transfers between devices: 0.01 us -> 9.41 us  [timed(): lax.all_to_all(out, 'frame', split_axis=0, concat_axis=0, tiled=True)]
    ppermute x1, waiting for transfers between devices: 18.4 us -> 11 us  [on_device(): prev_kv = lax.ppermute(to_next, 'frame', up)]
  transfers between devices with their start and end apart: 7 -> 11, of which waited for: 3 -> 5; matrix products, arithmetic and copies ran while one was open for 6% -> 6% of each run, Pallas kernels for 30% -> 49%
where the time goes in v2:
time: 211 us; the launch traced here: 208 us
  Pallas kernels  109 us (52%)
  starting transfers between devices  44.5 us (21%)
  waiting for transfers between devices  40.4 us (19%)
  local copies, waits for them, and re-layouts  8.27 us (4%)
  other arithmetic  5.51 us (3%)
    pallas_call x4, Pallas kernels, project(): pl.pallas_call(functools.partial(project_kernel, kinds, pair, near_count,...  57.9 us
    pallas_call x2, Pallas kernels, space_attend(): pl.pallas_call(functools.partial(space_attend_kernel, factor, parts), out...  32.3 us
    all_to_all x2, starting transfers between devices, timed(): lax.all_to_all(out, 'frame', split_axis=0, concat_axis=0, tiled=True)  21.1 us
    all_to_all x2, starting transfers between devices, on_device(): lax.all_to_all(packed, 'frame', split_axis=0, concat_axis=0, tiled=True)  11.3 us
    pallas_call x2, Pallas kernels, time_attend(): pl.pallas_call(functools.partial(time_attend_kernel, factor, mask.shape[1...  11.1 us
    ppermute x1, waiting for transfers between devices, on_device(): prev_kv = lax.ppermute(to_next, 'frame', up)  11 us
    ppermute x2, waiting for transfers between devices, on_device(): time_recv = lax.ppermute(time_send, 'head', swap)  10.4 us
    ppermute x2, waiting for transfers between devices, on_device(): recv = lax.ppermute(send, 'head', swap)  9.59 us
  transfers between devices with their start and end apart: 11, of which 5 were waited for; matrix products, arithmetic and copies ran while one was open for 6% of the time, Pallas kernels for 49%

profile of v2, /device:TPU:18, one launch (start us, length us, event | category | flops | bytes accessed | tf_op | source)
XLA Modules:
  0.0 207.7 jit_solution(16690184329497642191)
XLA Ops:
  0.0 0.8 reshape.151
  0.8 0.1 multiply_reduce_fusion.6
  0.9 0.6 collective-permute-start
  1.5 0.6 fusion.12
  2.1 11.4 %shard_map.73.after_ref = bf16[16,3,2,64,128]{4,3,2,1,0:T(8,128)(2,1)} custom-call(s32[2]{0:T(128)} %get-tuple-element.43.table, bf16[1024,3072]{1,0:T(8,128)(2,1)} %x_ref.7, f32[1,128]{1,0:T(1,128)} %bitcast.19, f32[1,128]{1,0:T(1,128)} %bitcast.24, f32[1,128]{1,0:T(1,128)} %bitcast.20, bf16[3,3072,1536]{2,1,0:T(8,128)(2,1)} %refs_1_.7, ...), custom_call_target="tpu_custom_call" | custom-call | flops 4831838208 | bytes 12582912 | tf_op jit(solution)/shard_map/pallas_call | solution.py:96
  13.5 6.2 %all-to-all-start = ((bf16[16,3,2,64,128]{4,3,2,1,0:T(8,128)(2,1)}), bf16[16,3,2,64,128]{4,3,2,1,0:T(8,128)(2,1)S(1)}, u32[]{:S(2)}, u32[]{:S(2)}) async-start(bf16[16,3,2,64,128]{4,3,2,1,0:T(8,128)(2,1)} %shard_map.73.after_ref), calls=%async_computation | async-start | bytes 3145728 | tf_op jit(solution)/shard_map/all_to_all | solution.py:385
  19.7 0.1 copy.22
  20.0 0.6 gather_fusion
  20.6 0.1 copy.24
  20.8 0.3 slice_reduce_fusion.1
  21.2 0.1 multiply_reduce_fusion.3
  21.3 0.2 fusion.2
  21.5 0.6 fusion.3
  22.1 0.1 reshape.157
  22.2 0.7 pad_add_fusion.2.table
  22.9 21.5 %shard_map.74 = (bf16[2,8,1024,128]{3,2,1,0:T(8,128)(2,1)}, bf16[2,8,512,128]{3,2,1,0:T(8,128)(2,1)}, bf16[2,8,512,128]{3,2,1,0:T(8,128)(2,1)}) custom-call(s32[136]{0:T(256)} %pad_add_fusion.2.table, bf16[1024,3072]{1,0:T(8,128)(2,1)} %x_ref.7, f32[1,128]{1,0:T(1,128)} %bitcast.21, f32[1,128]{1,0:T(1,128)} %bitcast.25, ...), custom_call_target="tpu_custom_call" | custom-call | flops 12884901888 | bytes 23068672 | tf_op jit(solution)/shard_map/pallas_call | solution.py:96
  44.4 2.0 collective-permute-start.1
  46.5 4.4 %collective-permute-start.2 = (bf16[2,8,512,128]{3,2,1,0:T(8,128)(2,1)}, bf16[2,8,512,128]{3,2,1,0:T(8,128)(2,1)}, u32[]{:S(2)}, u32[]{:S(2)}) collective-permute-start(bf16[2,8,512,128]{3,2,1,0:T(8,128)(2,1)} %get-tuple-element.18), channel_id=1, source_target_pairs={{2,0},{4,2},{6,4},{8,6},{10,8},{12,10},{14,12},{16,14},{18,16},{20... | collective-permute-start | bytes 6291464 | tf_op jit(solution)/shard_map/ppermute | solution.py:392
  50.9 11.4 %shard_map.75.after_ref = bf16[16,3,2,64,128]{4,3,2,1,0:T(8,128)(2,1)} custom-call(s32[2]{0:T(128)} %get-tuple-element.44.table, bf16[1024,3072]{1,0:T(8,128)(2,1)} %x_ref.7, f32[1,128]{1,0:T(1,128)} %bitcast.22, f32[1,128]{1,0:T(1,128)} %bitcast.26, bf16[2,8,1024,128]{3,2,1,0:T(8,128)(2,1)} %get-tuple-element.16.after_ref.kv_ref, ...), custom_call_target="tpu_custom_call" | custom-call | flops 4831838208 | bytes 12582912 | tf_op jit(solution)/shard_map/pallas_call | solution.py:96
  62.4 5.1 %all-to-all-start.2 = ((bf16[16,3,2,64,128]{4,3,2,1,0:T(8,128)(2,1)}), bf16[16,3,2,64,128]{4,3,2,1,0:T(8,128)(2,1)S(1)}, u32[]{:S(2)}, u32[]{:S(2)}) async-start(bf16[16,3,2,64,128]{4,3,2,1,0:T(8,128)(2,1)} %shard_map.75.after_ref), calls=%async_computation.2 | async-start | bytes 3145728 | tf_op jit(solution)/shard_map/all_to_all | solution.py:385
  67.5 0.1 copy.28
  67.6 0.6 gather_fusion.1
  68.3 0.7 reshape.159.mask
  68.9 0.7 reshape.158.mask
  69.8 1.2 multiply_reduce_fusion.1
  70.9 1.9 multiply_reduce_fusion
  72.9 0.7 pad.4.bias_ref
  73.6 13.5 %shard_map.76.after_ref.q_ref = bf16[1,8,1024,128]{3,2,1,0:T(8,128)(2,1)} custom-call(s32[8]{0:T(128)} %copy-done.7, bf16[1024,3072]{1,0:T(8,128)(2,1)} %x_ref.7, f32[1,128]{1,0:T(1,128)} %bitcast.23, f32[1,128]{1,0:T(1,128)} %bitcast.27, bf16[16,3,2,64,128]{4,3,2,1,0:T(8,128)(2,1)} %shard_map.75.after_ref, bf16[3,3072,1536]{2,1,0:T(8,128)(2,1)} %refs_1_.7, ...), custom_call_target="tpu_custom_call" | custom-call | flops 6442450944 | bytes 14680064 | tf_op jit(solution)/shard_map/pallas_call | solution.py:96
  87.1 5.5 %time_attend.2.after_ref = bf16[16,2,64,128]{3,2,1,0:T(8,128)(2,1)} custom-call(s32[8]{0:T(128)} %reshape.158.mask, bf16[16,3,2,64,128]{4,3,2,1,0:T(8,128)(2,1)} %copy-done.1, bf16[1,8,1024,128]{3,2,1,0:T(8,128)(2,1)} %shard_map.76.after_ref.q_ref), custom_call_target="tpu_custom_call" | custom-call | flops 2147483648 | bytes 2097152 | tf_op jit(solution)/shard_map/time_attend/pallas_call | solution.py:248
  92.6 11.0 %collective-permute-done.1.prev_ref = bf16[2,8,512,128]{3,2,1,0:T(8,128)(2,1)} collective-permute-done((bf16[2,8,512,128]{3,2,1,0:T(8,128)(2,1)}, bf16[2,8,512,128]{3,2,1,0:T(8,128)(2,1)}, u32[]{:S(2)}, u32[]{:S(2)}) %collective-permute-start.1) | collective-permute-done | bytes 2097184 | tf_op jit(solution)/shard_map/ppermute | solution.py:391
  103.7 16.2 %shard_map.77 = (bf16[4,512,128]{2,1,0:T(8,128)(2,1)}, bf16[4,512,128]{2,1,0:T(8,128)(2,1)}) custom-call(s32[1]{0:T(128)} %bitcast.4.side, bf16[1,8,1024,128]{3,2,1,0:T(8,128)(2,1)} %shard_map.76.after_ref.q_ref, bf16[2,8,1024,128]{3,2,1,0:T(8,128)(2,1)} %get-tuple-element.16.after_ref.kv_ref, bf16[2,8,512,128]{3,2,1,0:T(8,128)(2,1)} %collective-permute-done.1.prev_ref, ...), custom_call_target="tpu_custom_call" | custom-call | flops 8589934592 | bytes 6291456 | tf_op jit(solution)/shard_map/pallas_call | solution.py:185
  119.8 15.1 %all-to-all-start.1 = ((bf16[16,2,64,128]{3,2,1,0:T(8,128)(2,1)}), bf16[16,2,64,128]{3,2,1,0:T(8,128)(2,1)S(1)}, u32[]{:S(2)}, u32[]{:S(2)}) async-start(bf16[16,2,64,128]{3,2,1,0:T(8,128)(2,1)} %time_attend.2.after_ref), calls=%async_computation.1 | async-start | bytes 1048576 | tf_op jit(solution)/shard_map/all_to_all | solution.py:405
  134.9 16.2 %shard_map.78 = (bf16[4,512,128]{2,1,0:T(8,128)(2,1)}, bf16[4,512,128]{2,1,0:T(8,128)(2,1)}) custom-call(s32[1]{0:T(128)} %bitcast.4.side, bf16[1,8,1024,128]{3,2,1,0:T(8,128)(2,1)} %shard_map.76.after_ref.q_ref, bf16[2,8,1024,128]{3,2,1,0:T(8,128)(2,1)} %get-tuple-element.16.after_ref.kv_ref, bf16[2,8,512,128]{3,2,1,0:T(8,128)(2,1)} %collective-permute-done.1.prev_ref, ...), custom_call_target="tpu_custom_call" | custom-call | flops 8589934592 | bytes 6291456 | tf_op jit(solution)/shard_map/pallas_call | solution.py:185
  151.1 5.6 %time_attend.3 = bf16[16,2,64,128]{3,2,1,0:T(8,128)(2,1)} custom-call(s32[8]{0:T(128)} %reshape.159.mask, bf16[16,3,2,64,128]{4,3,2,1,0:T(8,128)(2,1)} %copy-done.2, bf16[4,512,128]{2,1,0:T(8,128)(2,1)} %get-tuple-element.21.after_ref.refs_4_), custom_call_target="tpu_custom_call" | custom-call | flops 2147483648 | bytes 2097152 | tf_op jit(solution)/shard_map/time_attend/pallas_call | solution.py:248
  156.8 6.0 %all-to-all-start.3 = ((bf16[16,2,64,128]{3,2,1,0:T(8,128)(2,1)}), bf16[16,2,64,128]{3,2,1,0:T(8,128)(2,1)S(1)}, u32[]{:S(2)}, u32[]{:S(2)}) async-start(bf16[16,2,64,128]{3,2,1,0:T(8,128)(2,1)} %time_attend.3), calls=%async_computation.3 | async-start | bytes 1048576 | tf_op jit(solution)/shard_map/all_to_all | solution.py:405
  163.0 1.5 collective-permute-start.5
  164.5 0.5 collective-permute-start.3
  165.0 0.8 constant_dynamic-slice_fusion.2
  165.8 1.5 collective-permute-start.4
  167.2 9.4 %all-to-all-done.3 = bf16[16,2,64,128]{3,2,1,0:T(8,128)(2,1)S(1)} async-done(((bf16[16,2,64,128]{3,2,1,0:T(8,128)(2,1)}), bf16[16,2,64,128]{3,2,1,0:T(8,128)(2,1)S(1)}, u32[]{:S(2)}, u32[]{:S(2)}) %all-to-all-start.3) | async-done | bytes 524320 | tf_op jit(solution)/shard_map/all_to_all | solution.py:405
  176.7 0.8 constant_dynamic-slice_fusion
  177.4 1.5 collective-permute-start.6
  179.0 0.6 concatenate.17.table
  179.6 9.6 %collective-permute-done.3.refs_2_ = bf16[4,512,128]{2,1,0:T(8,128)(2,1)S(1)} collective-permute-done((bf16[4,512,128]{2,1,0:T(8,128)(2,1)S(1)}, bf16[4,512,128]{2,1,0:T(8,128)(2,1)S(1)}, u32[]{:S(2)}, u32[]{:S(2)}) %collective-permute-start.3) | collective-permute-done | bytes 524320 | tf_op jit(solution)/shard_map/ppermute | solution.py:431
  189.2 5.6 %collective-permute-done.4.refs_3_ = bf16[8,2,64,128]{3,2,1,0:T(8,128)(2,1)S(1)} collective-permute-done((bf16[8,2,64,128]{3,2,1,0:T(8,128)(2,1)S(1)}, bf16[8,2,64,128]{3,2,1,0:T(8,128)(2,1)S(1)}, u32[]{:S(2)}, u32[]{:S(2)}) %collective-permute-start.4) | collective-permute-done | bytes 262176 | tf_op jit(solution)/shard_map/ppermute | solution.py:434
  194.8 4.8 %collective-permute-done.6.refs_7_ = bf16[8,2,64,128]{3,2,1,0:T(8,128)(2,1)S(1)} collective-permute-done((bf16[8,2,64,128]{3,2,1,0:T(8,128)(2,1)S(1)}, bf16[8,2,64,128]{3,2,1,0:T(8,128)(2,1)S(1)}, u32[]{:S(2)}, u32[]{:S(2)}) %collective-permute-start.6) | collective-permute-done | bytes 262176 | tf_op jit(solution)/shard_map/ppermute | solution.py:434
  199.6 0.7 copy-done.6
  200.3 7.4 %assemble.1 = bf16[512,3072]{1,0:T(8,128)(2,1)} custom-call(s32[80]{0:T(128)} %concatenate.17.table, bf16[4,512,128]{2,1,0:T(8,128)(2,1)} %get-tuple-element.19.after_ref.refs_0_, bf16[8,2,64,128]{3,2,1,0:T(8,128)(2,1)} %get-tuple-element.30.refs_1_, bf16[4,512,128]{2,1,0:T(8,128)(2,1)} %copy-done.4, bf16[8,2,64,128]{3,2,1,0:T(8,128)(2,1)} %copy-done.5, ...), custom_call_target="tpu_custom_call" | custom-call | bytes 6291456 | tf_op jit(solution)/shard_map/assemble/pallas_call | solution.py:309
  (53 shorter events, 0.9 us)
Async XLA Ops:
  0.0 20.0 %copy-start = (s32[12,16,48]{2,1,0:T(8,128)S(1)}, s32[12,16,48]{2,1,0:T(8,128)}, u32[]{:S(2)}) copy-start(s32[12,16,48]{2,1,0:T(8,128)} %param.12) | copy-start | bytes 110596
  0.9 21.2 %collective-permute-start = (s32[4]{0:T(128)S(1)}, s32[4]{0:T(128)S(1)}, u32[]{:S(2)}, u32[]{:S(2)}) collective-permute-start(s32[4]{0:T(128)S(1)} %multiply_reduce_fusion.6), channel_id=1, source_target_pairs={{0,1},{1,0},{2,3},{3,2},{4,5},{5,4},{6,7},{7,6},{8,9},{9,8},{10,11... | collective-permute-start | bytes 56 | tf_op jit(solution)/shard_map/ppermute | solution.py:371
  13.5 48.8 %all-to-all-start = ((bf16[16,3,2,64,128]{4,3,2,1,0:T(8,128)(2,1)}), bf16[16,3,2,64,128]{4,3,2,1,0:T(8,128)(2,1)S(1)}, u32[]{:S(2)}, u32[]{:S(2)}) async-start(bf16[16,3,2,64,128]{4,3,2,1,0:T(8,128)(2,1)} %shard_map.73.after_ref), calls=%async_computation | async-start | bytes 3145728 | tf_op jit(solution)/shard_map/all_to_all | solution.py:385
  19.9 24.5 %copy-start.7 = (s32[8]{0:T(128)}, s32[8]{0:T(128)S(1)}, u32[]{:S(2)}) copy-start(s32[8]{0:T(128)S(1)} %reshape.152.table) | copy-start | bytes 100
  44.4 59.2 %collective-permute-start.1 = (bf16[2,8,512,128]{3,2,1,0:T(8,128)(2,1)}, bf16[2,8,512,128]{3,2,1,0:T(8,128)(2,1)}, u32[]{:S(2)}, u32[]{:S(2)}) collective-permute-start(bf16[2,8,512,128]{3,2,1,0:T(8,128)(2,1)} %get-tuple-element.17), channel_id=1, source_target_pairs={{0,2},{2,4},{4,6},{6,8},{8,10},{10,12},{12,14},{14,16},{16,18},{18... | collective-permute-start | bytes 6291464 | tf_op jit(solution)/shard_map/ppermute | solution.py:391
  46.5 57.2 %collective-permute-start.2 = (bf16[2,8,512,128]{3,2,1,0:T(8,128)(2,1)}, bf16[2,8,512,128]{3,2,1,0:T(8,128)(2,1)}, u32[]{:S(2)}, u32[]{:S(2)}) collective-permute-start(bf16[2,8,512,128]{3,2,1,0:T(8,128)(2,1)} %get-tuple-element.18), channel_id=1, source_target_pairs={{2,0},{4,2},{6,4},{8,6},{10,8},{12,10},{14,12},{16,14},{18,16},{20... | collective-permute-start | bytes 6291464 | tf_op jit(solution)/shard_map/ppermute | solution.py:392
  62.3 5.2 %copy-start.8 = (s32[12,2,2]{0,2,1:T(2,128)S(1)}, s32[12,2,2]{0,2,1:T(2,128)}, u32[]{:S(2)}) copy-start(s32[12,2,2]{0,2,1:T(2,128)} %param.13) | copy-start | bytes 580
  62.3 11.2 %copy-start.1 = (bf16[16,3,2,64,128]{4,3,2,1,0:T(8,128)(2,1)}, bf16[16,3,2,64,128]{4,3,2,1,0:T(8,128)(2,1)S(1)}, u32[]{:S(2)}) copy-start(bf16[16,3,2,64,128]{4,3,2,1,0:T(8,128)(2,1)S(1)} %all-to-all-done.x_ref) | copy-start | bytes 4718596
  62.4 57.5 %all-to-all-start.2 = ((bf16[16,3,2,64,128]{4,3,2,1,0:T(8,128)(2,1)}), bf16[16,3,2,64,128]{4,3,2,1,0:T(8,128)(2,1)S(1)}, u32[]{:S(2)}, u32[]{:S(2)}) async-start(bf16[16,3,2,64,128]{4,3,2,1,0:T(8,128)(2,1)} %shard_map.75.after_ref), calls=%async_computation.2 | async-start | bytes 3145728 | tf_op jit(solution)/shard_map/all_to_all | solution.py:385
  119.8 31.3 %copy-start.2 = (bf16[16,3,2,64,128]{4,3,2,1,0:T(8,128)(2,1)}, bf16[16,3,2,64,128]{4,3,2,1,0:T(8,128)(2,1)S(1)}, u32[]{:S(2)}) copy-start(bf16[16,3,2,64,128]{4,3,2,1,0:T(8,128)(2,1)S(1)} %all-to-all-done.2.x_ref) | copy-start | bytes 4718596
  119.8 36.9 %all-to-all-start.1 = ((bf16[16,2,64,128]{3,2,1,0:T(8,128)(2,1)}), bf16[16,2,64,128]{3,2,1,0:T(8,128)(2,1)S(1)}, u32[]{:S(2)}, u32[]{:S(2)}) async-start(bf16[16,2,64,128]{3,2,1,0:T(8,128)(2,1)} %time_attend.2.after_ref), calls=%async_computation.1 | async-start | bytes 1048576 | tf_op jit(solution)/shard_map/all_to_all | solution.py:405
  151.1 13.3 %copy-start.9 = (bf16[4,512,128]{2,1,0:T(8,128)(2,1)S(1)}, bf16[4,512,128]{2,1,0:T(8,128)(2,1)}, u32[]{:S(2)}) copy-start(bf16[4,512,128]{2,1,0:T(8,128)(2,1)} %get-tuple-element.20) | copy-start | bytes 1572868
  156.8 19.9 %all-to-all-start.3 = ((bf16[16,2,64,128]{3,2,1,0:T(8,128)(2,1)}), bf16[16,2,64,128]{3,2,1,0:T(8,128)(2,1)S(1)}, u32[]{:S(2)}, u32[]{:S(2)}) async-start(bf16[16,2,64,128]{3,2,1,0:T(8,128)(2,1)} %time_attend.3), calls=%async_computation.3 | async-start | bytes 1048576 | tf_op jit(solution)/shard_map/all_to_all | solution.py:405
  163.0 16.7 %collective-permute-start.5 = (bf16[4,512,128]{2,1,0:T(8,128)(2,1)}, bf16[4,512,128]{2,1,0:T(8,128)(2,1)S(1)}, u32[]{:S(2)}, u32[]{:S(2)}) collective-permute-start(bf16[4,512,128]{2,1,0:T(8,128)(2,1)} %get-tuple-element.22), channel_id=1, source_target_pairs={{0,1},{1,0},{2,3},{3,2},{4,5},{5,4},{6,7},{7,6},{8,9},{9,8},{10,11... | collective-permute-start | bytes 1572872 | tf_op jit(solution)/shard_map/ppermute | solution.py:431
  164.5 24.8 %collective-permute-start.3 = (bf16[4,512,128]{2,1,0:T(8,128)(2,1)S(1)}, bf16[4,512,128]{2,1,0:T(8,128)(2,1)S(1)}, u32[]{:S(2)}, u32[]{:S(2)}) collective-permute-start(bf16[4,512,128]{2,1,0:T(8,128)(2,1)S(1)} %copy-done.9), channel_id=1, source_target_pairs={{0,1},{1,0},{2,3},{3,2},{4,5},{5,4},{6,7},{7,6},{8,9},{9,8},{10,11... | collective-permute-start | bytes 1572872 | tf_op jit(solution)/shard_map/ppermute | solution.py:431
  165.8 29.1 %collective-permute-start.4 = (bf16[8,2,64,128]{3,2,1,0:T(8,128)(2,1)S(1)}, bf16[8,2,64,128]{3,2,1,0:T(8,128)(2,1)S(1)}, u32[]{:S(2)}, u32[]{:S(2)}) collective-permute-start(bf16[8,2,64,128]{3,2,1,0:T(8,128)(2,1)S(1)} %get-tuple-element.29), channel_id=1, source_target_pairs={{0,1},{1,0},{2,3},{3,2},{4,5},{5,4},{6,7},{7,6},{8,9},{9,8},{10,11... | collective-permute-start | bytes 786440 | tf_op jit(solution)/shard_map/ppermute | solution.py:434
  177.4 22.2 %collective-permute-start.6 = (bf16[8,2,64,128]{3,2,1,0:T(8,128)(2,1)S(1)}, bf16[8,2,64,128]{3,2,1,0:T(8,128)(2,1)S(1)}, u32[]{:S(2)}, u32[]{:S(2)}) collective-permute-start(bf16[8,2,64,128]{3,2,1,0:T(8,128)(2,1)S(1)} %get-tuple-element.27), channel_id=1, source_target_pairs={{0,1},{1,0},{2,3},{3,2},{4,5},{5,4},{6,7},{7,6},{8,9},{9,8},{10,11... | collective-permute-start | bytes 786440 | tf_op jit(solution)/shard_map/ppermute | solution.py:434
  179.6 20.0 %copy-start.3 = (bf16[4,512,128]{2,1,0:T(8,128)(2,1)}, bf16[4,512,128]{2,1,0:T(8,128)(2,1)S(1)}, u32[]{:S(2)}) copy-start(bf16[4,512,128]{2,1,0:T(8,128)(2,1)S(1)} %collective-permute-done.5.refs_6_) | copy-start | bytes 1572868
  189.2 10.4 %copy-start.4 = (bf16[4,512,128]{2,1,0:T(8,128)(2,1)}, bf16[4,512,128]{2,1,0:T(8,128)(2,1)S(1)}, u32[]{:S(2)}) copy-start(bf16[4,512,128]{2,1,0:T(8,128)(2,1)S(1)} %collective-permute-done.3.refs_2_) | copy-start | bytes 1572868
  194.8 4.8 %copy-start.5 = (bf16[8,2,64,128]{3,2,1,0:T(8,128)(2,1)}, bf16[8,2,64,128]{3,2,1,0:T(8,128)(2,1)S(1)}, u32[]{:S(2)}) copy-start(bf16[8,2,64,128]{3,2,1,0:T(8,128)(2,1)S(1)} %collective-permute-done.4.refs_3_) | copy-start | bytes 786436
  199.6 0.7 copy-start.6

commit v3 on v2

--- a/solution.py
+++ b/solution.py
@@ -35,7 +35,7 @@
     out_ref = outs[0]
     i = pl.program_id(0)
     count = pl.num_programs(0) * pair
-    step = chunk_rows(x_ref.shape[0], 512)
+    step = x_ref.shape[0] // strips if strips > 1 else chunk_rows(x_ref.shape[0], 512)
     gains = {0: gq_ref[...], 1: gk_ref[...]}
 
     def body(m, carry):
@@ -53,8 +53,13 @@
                     part = part.astype(jnp.bfloat16)
                 if strips:
                     pos = out_ref.shape[3]
-                    per = step // pos
-                    out_ref[pl.ds(m * per, per), n, j] = part.reshape(per, pos, HD)
+                    if strips == 1:
+                        per = step // pos
+                        out_ref[pl.ds(m * per, per), n, j] = part.reshape(per, pos, HD)
+                    else:
+                        q = pos // strips
+                        at = pl.ds(pl.multiple_of(m * q, q), q)
+                        out_ref[:, n, j, at, :] = part.reshape(out_ref.shape[0], q, HD)
                 else:
                     out_ref[n, j, rows, :] = part
         return carry
@@ -70,7 +75,7 @@
                     ref[n, j, s * BLOCK : (s + 1) * BLOCK, :] = out_ref[n, j, src, :]
 
 
-def project(tokens, weight, gq, gk, heads, kinds, after, strips=0, picks=None):
+def project(tokens, weight, gq, gk, heads, kinds, after, strips=0, deal=1, picks=None):
     rows, d = tokens.shape
     count = heads.shape[0]
     pair = 2 if count % 2 == 0 else 1
@@ -94,7 +99,7 @@
         shapes += [jax.ShapeDtypeStruct((2, count, near, HD), jnp.bfloat16)] * 2
         specs += [pl.BlockSpec((2, pair, near, HD), lambda i, t: (0, i, 0, 0))] * 2
     out = pl.pallas_call(
-        functools.partial(project_kernel, kinds, pair, near_count, bool(strips)),
+        functools.partial(project_kernel, kinds, pair, near_count, deal if strips else 0),
         out_shape=tuple(shapes),
         grid_spec=pltpu.PrefetchScalarGridSpec(
             num_scalar_prefetch=1,
@@ -127,8 +132,7 @@
     return (both[:, :HD] / both[:, HD:]).astype(jnp.bfloat16)
 
 
-def space_attend_kernel(factor, parts, side, q_ref, kv_ref, prev_ref, next_ref, bias_ref, after_ref, *refs):
-    outs, (ka, va, marks) = refs[:-3], refs[-3:]
+def space_attend_kernel(factor, parts, side, q_ref, kv_ref, prev_ref, next_ref, bias_ref, after_ref, out_ref, ka, va, marks):
     rows = q_ref.shape[0]
     near = prev_ref.shape[1]
     total = rows + 2 * near
@@ -154,49 +158,34 @@
         span = slice(m * step, (m + 1) * step)
         queries = jnp.concatenate([q_ref[span, :], marks[span, :]], axis=1)
         result = attend_rows(queries, ka[...], va[...], factor)
-        half = m * step // part
-        rest = slice(m * step % part, m * step % part + step)
-        if len(outs) == 1:
-            outs[0][half, rest, :] = result
-        else:
-
-            @pl.when(side[0] == half)
-            def _():
-                outs[0][rest, :] = result
-
-            @pl.when(side[0] != half)
-            def _():
-                outs[1][rest, :] = result
-
-
-def space_attend(q, kv, prev_kv, next_kv, bias, first, count, parts, side, after):
+        which = lax.rem(m * step // part - side[0] + parts, parts)
+        first = m * step % part
+        out_ref[which, first : first + step, :] = result
+
+
+def space_attend(q, kv, prev_kv, next_kv, bias, parts, side, after):
+    count = q.shape[1]
     rows = q.shape[2]
     near = prev_kv.shape[2]
     total = rows + 2 * near
     factor = math.log2(math.e) / math.sqrt(HD)
-    near_spec = pl.BlockSpec((2, None, near, HD), lambda h, t: (0, first + h, 0, 0))
+    near_spec = pl.BlockSpec((2, None, near, HD), lambda h, t: (0, h, 0, 0))
     part = rows // parts
-    if parts == 2:
-        shapes = [jax.ShapeDtypeStruct((count, part, HD), jnp.bfloat16)] * 2
-        specs = [pl.BlockSpec((None, part, HD), lambda h, t: (h, 0, 0))] * 2
-    else:
-        shapes = [jax.ShapeDtypeStruct((parts, count, part, HD), jnp.bfloat16)]
-        specs = [pl.BlockSpec((parts, None, part, HD), lambda h, t: (0, h, 0, 0))]
     return pl.pallas_call(
         functools.partial(space_attend_kernel, factor, parts),
-        out_shape=tuple(shapes),
+        out_shape=jax.ShapeDtypeStruct((parts, count, part, HD), jnp.bfloat16),
         grid_spec=pltpu.PrefetchScalarGridSpec(
             num_scalar_prefetch=1,
             grid=(count,),
             in_specs=[
-                pl.BlockSpec((None, None, rows, HD), lambda h, t: (0, first + h, 0, 0)),
-                pl.BlockSpec((2, None, rows, HD), lambda h, t: (0, first + h, 0, 0)),
+                pl.BlockSpec((None, None, rows, HD), lambda h, t: (0, h, 0, 0)),
+                pl.BlockSpec((2, None, rows, HD), lambda h, t: (0, h, 0, 0)),
                 near_spec,
                 near_spec,
-                pl.BlockSpec((None, total // BLOCK, HD), lambda h, t: (first + h, 0, 0)),
+                pl.BlockSpec((None, total // BLOCK, HD), lambda h, t: (h, 0, 0)),
                 pl.BlockSpec(memory_space=pl.ANY),
             ],
-            out_specs=tuple(specs),
+            out_specs=pl.BlockSpec((parts, None, part, HD), lambda h, t: (0, h, 0, 0)),
             scratch_shapes=[
                 pltpu.VMEM((total, 2 * HD), jnp.bfloat16),
                 pltpu.VMEM((total, 2 * HD), jnp.bfloat16),
@@ -209,6 +198,7 @@
             bytes_accessed=2 * HD * count * (4 * rows + 4 * near),
             transcendentals=count * rows * total,
         ),
+        name="space_attend",
     )(side, q, kv, prev_kv, next_kv, bias, after)
 
 
@@ -236,18 +226,19 @@
     queries = jnp.concatenate([x_ref[:, 0].reshape(rows, HD), marks], axis=1)
     step = chunk_rows(rows, 256)
     per = step // pos
+    parts, q = out_ref.shape[1], out_ref.shape[2]
     for m in range(rows // step):
         result = attend_rows(queries[m * step : (m + 1) * step], ka[...], va[...], factor)
-        out_ref[m * per : (m + 1) * per] = result.reshape(per, pos, HD)
-
-
-def time_attend(received, mask, after):
+        out_ref[m * per : (m + 1) * per] = result.reshape(per, parts, q, HD)
+
+
+def time_attend(received, mask, after, deal):
     frames, _, count, pos, _ = received.shape
     rows = frames * pos
     factor = math.log2(math.e) / math.sqrt(HD)
     return pl.pallas_call(
         functools.partial(time_attend_kernel, factor, mask.shape[1]),
-        out_shape=jax.ShapeDtypeStruct((frames, count, pos, HD), jnp.bfloat16),
+        out_shape=jax.ShapeDtypeStruct((frames, deal, count, pos // deal, HD), jnp.bfloat16),
         grid_spec=pltpu.PrefetchScalarGridSpec(
             num_scalar_prefetch=1,
             grid=(count,),
@@ -255,7 +246,7 @@
                 pl.BlockSpec((frames, 3, None, pos, HD), lambda h, t: (0, 0, h, 0, 0)),
                 pl.BlockSpec(memory_space=pl.ANY),
             ],
-            out_specs=pl.BlockSpec((frames, None, pos, HD), lambda h, t: (0, h, 0, 0)),
+            out_specs=pl.BlockSpec((frames, deal, None, pos // deal, HD), lambda h, t: (0, 0, h, 0, 0)),
             scratch_shapes=[
                 pltpu.VMEM((rows, 2 * HD), jnp.bfloat16),
                 pltpu.VMEM((rows, 2 * HD), jnp.bfloat16),
@@ -271,55 +262,59 @@
     )(mask.reshape(-1), received, after)
 
 
-def assemble_kernel(sources, table, *refs):
-    g = pl.program_id(0)
-    groups = pl.num_programs(0)
+def place_space_kernel(sources, table, *refs):
+    h = pl.program_id(0)
+    chosen = table[pl.num_programs(0) + h]
     out_ref = refs[-1]
-    slot, chosen = table[g], table[groups + g]
-    rows = out_ref.shape[0]
     for n in range(sources):
-        s_ref, t_ref = refs[2 * n], refs[2 * n + 1]
-        for want in range(3):
-
-            @pl.when((chosen == n) & (slot == want))
-            def _():
-                order = [s_ref[0], s_ref[1]]
-                order.insert(want, t_ref[...].reshape(rows, HD))
-                for c in range(3):
-                    out_ref[:, c * HD : (c + 1) * HD] = order[c]
-
-
-def assemble(slots, chosen, sources, chunks):
-    groups = slots.shape[0]
+
+        @pl.when(chosen == n)
+        def _():
+            out_ref[...] = refs[n][...]
+
+
+def place_space(columns, chosen, sources, width):
+    count = columns.shape[0]
     rows = sources[0][0].shape[1]
-    tables, specs, arrays = [slots, chosen], [], []
-    for n, (space, timed, side, at) in enumerate(sources):
-        per = timed.shape[1]
-        pos = timed.shape[2]
-        tables += [side, at]
-
-        def space_index(g, t, n=n, per=per):
-            return (t[(2 + 2 * n) * groups + g] * per + t[(3 + 2 * n) * groups + g], 0, 0)
-
-        def time_index(g, t, n=n):
-            return (t[(2 + 2 * n) * groups + g], t[(3 + 2 * n) * groups + g], 0, 0)
-
-        specs += [pl.BlockSpec((2, rows, HD), space_index), pl.BlockSpec((chunks, None, pos, HD), time_index)]
-        arrays += [space, timed]
+
+    def spec(n):
+        return pl.BlockSpec((None, rows, HD), lambda h, t: (t[(2 + n) * count + h], 0, 0))
+
     return pl.pallas_call(
-        functools.partial(assemble_kernel, len(sources)),
-        out_shape=jax.ShapeDtypeStruct((rows, groups * 3 * HD), jnp.bfloat16),
+        functools.partial(place_space_kernel, len(sources)),
+        out_shape=jax.ShapeDtypeStruct((rows, width), jnp.bfloat16),
         grid_spec=pltpu.PrefetchScalarGridSpec(
             num_scalar_prefetch=1,
-            grid=(groups,),
-            in_specs=specs,
-            out_specs=pl.BlockSpec((rows, 3 * HD), lambda g, t: (0, g)),
-        ),
+            grid=(count,),
+            in_specs=[spec(n) for n in range(len(sources))],
+            out_specs=pl.BlockSpec((rows, HD), lambda h, t: (0, t[h])),
+        ),
+        cost_estimate=pl.CostEstimate(flops=0, bytes_accessed=4 * rows * count * HD, transcendentals=0),
+        name="place_space",
+    )(jnp.concatenate([columns, chosen] + [at for _, at in sources]), *[array for array, _ in sources])
+
+
+def place_time_kernel(table, timed_ref, placed_ref, out_ref):
+    out_ref[...] = timed_ref[...].reshape(out_ref.shape)
+
+
+def place_time(columns, timed, block, index, placed):
+    rows = placed.shape[0]
+    return pl.pallas_call(
+        place_time_kernel,
+        out_shape=jax.ShapeDtypeStruct(placed.shape, placed.dtype),
+        grid_spec=pltpu.PrefetchScalarGridSpec(
+            num_scalar_prefetch=1,
+            grid=(columns.shape[0],),
+            in_specs=[pl.BlockSpec(block, index), pl.BlockSpec(memory_space=pl.ANY)],
+            out_specs=pl.BlockSpec((rows, HD), lambda g, t: (0, t[g])),
+        ),
+        input_output_aliases={2: 0},
         cost_estimate=pl.CostEstimate(
-            flops=0, bytes_accessed=4 * rows * groups * 3 * HD, transcendentals=0
-        ),
-        name="assemble",
-    )(jnp.concatenate(tables), *arrays)
+            flops=0, bytes_accessed=4 * rows * columns.shape[0] * HD, transcendentals=0
+        ),
+        name="place_time",
+    )(columns, timed, placed)
 
 
 def block_picks(live):
@@ -366,87 +361,79 @@
     )
     bias = jnp.pad((allowed.astype(jnp.float32) - 1.0) * BIG, ((0, 0), (0, 0), (0, HD - blocks)))
 
+    pos_count = row_count // frame_count
+    deal = sides if pos_count % (sides * STRIP) == 0 else 1
+    up = [(i, i + 1) for i in range(frame_count - 1)]
+    down = [(i + 1, i) for i in range(frame_count - 1)]
     swap = [(0, 1), (1, 0)]
+    kv, to_next, to_prev = project(tokens, qkv_weight, gq, gk, space_heads, (1, 2), gq, picks=picks)
+    prev_kv = lax.ppermute(to_next, "frame", up)
+    next_kv = lax.ppermute(to_prev, "frame", down)
+    packed = project(tokens, qkv_weight, gq, gk, time_heads, (0, 1, 2), kv, strips=frame_count, deal=deal)
+    received = lax.all_to_all(packed, "frame", split_axis=0, concat_axis=0, tiled=True)
+    query_heads = space_heads
     if sides == 2:
         their_slot = lax.ppermute(time_slot, "head", swap)
-        picks, their_slot = lax.optimization_barrier((picks, their_slot))
-
-    splits = 2 if groups % 2 == 0 else 1
-    share = groups // splits
-    up = [(i, i + 1) for i in range(frame_count - 1)]
-    down = [(i + 1, i) for i in range(frame_count - 1)]
-    received = []
-    after = gq
-    for n in range(splits):
-        packed = project(
-            tokens, qkv_weight, gq, gk, time_heads[n * share : (n + 1) * share], (0, 1, 2), after,
-            strips=frame_count,
-        )
-        received.append(lax.all_to_all(packed, "frame", split_axis=0, concat_axis=0, tiled=True))
-        after = packed
-        if n == 0:
-            kv, to_next, to_prev = project(
-                tokens, qkv_weight, gq, gk, space_heads, (1, 2), after, picks=picks
-            )
-            prev_kv = lax.ppermute(to_next, "frame", up)
-            next_kv = lax.ppermute(to_prev, "frame", down)
-            after = kv
-    space_q = project(tokens, qkv_weight, gq, gk, space_heads, (0,), after)
-
-    mask = jnp.take(time_mask, time_heads, axis=0)
-    side = jnp.reshape(own_side, (1,)).astype(jnp.int32)
-    part_rows = row_count // sides
-    chunks = frame_count // sides
-    after = space_q
-    returned, space_out = [], []
-
-    def timed(n, after):
-        out = time_attend(received[n], mask[n * share : (n + 1) * share], after)
-        returned.append(lax.all_to_all(out, "frame", split_axis=0, concat_axis=0, tiled=True))
-        return out
-
-    if splits == 2:
-        after = timed(0, after)
-    for n in range(splits):
-        out = space_attend(
-            space_q, kv, prev_kv, next_kv, bias, n * 2 * share, 2 * share, sides, side, after
-        )
-        space_out.append(out)
-        after = out[0]
-    timed(splits - 1, after)
-
-    side_ids = jnp.repeat(jnp.arange(sides, dtype=jnp.int32), groups)
-    group_ids = jnp.tile(jnp.arange(groups, dtype=jnp.int32), sides)
-    all_ids = jnp.arange(sides * groups, dtype=jnp.int32)
-    zeros = jnp.zeros_like(side_ids)
-    sources = []
-    if sides == 2:
+        query_heads, their_slot = lax.optimization_barrier((space_heads, their_slot))
         slots = jnp.where(
             own_side == 0,
             jnp.concatenate([time_slot, their_slot]),
             jnp.concatenate([their_slot, time_slot]),
         )
-        for n in range(splits):
-            keep, send = space_out[n]
-            recv = lax.ppermute(send, "head", swap)
-            time_keep = lax.dynamic_slice_in_dim(returned[n], own_side * chunks, chunks, 0)
-            time_send = lax.dynamic_slice_in_dim(returned[n], (1 - own_side) * chunks, chunks, 0)
-            time_recv = lax.ppermute(time_send, "head", swap)
-            for whose, space_part, time_part in ((own_side, keep, time_keep), (1 - own_side, recv, time_recv)):
-                at = jnp.clip(all_ids - whose * groups - n * share, 0, share - 1)
-                sources.append((space_part, time_part, zeros, at))
-        chosen = group_ids // share * 2 + (side_ids != own_side).astype(jnp.int32)
     else:
         slots = lax.all_to_all(
             jnp.broadcast_to(time_slot[None], (sides, groups)), "head", 0, 0, tiled=True
         ).reshape(-1)
-        for n in range(splits):
-            space_part = lax.all_to_all(space_out[n][0], "head", 0, 0, tiled=True)
-            time_part = lax.all_to_all(returned[n], "head", 0, 0, tiled=True)
-            at = jnp.clip(group_ids - n * share, 0, share - 1)
-            sources.append((space_part.reshape(-1, part_rows, HD), time_part, side_ids, at))
-        chosen = group_ids // share
-    return assemble(slots, chosen, sources, chunks)
+    space_q = project(tokens, qkv_weight, gq, gk, query_heads, (0,), packed)
+
+    side = jnp.reshape(own_side if sides == 2 else jnp.int32(0), (1,)).astype(jnp.int32)
+    space_out = space_attend(space_q, kv, prev_kv, next_kv, bias, sides, side, space_q)
+    mask = jnp.take(time_mask, time_heads, axis=0)
+    time_out = time_attend(received, mask, space_out, deal)
+
+    part_rows = row_count // sides
+    total_heads = sides * space_count
+    head_ids = jnp.arange(total_heads, dtype=jnp.int32)
+    if sides == 2:
+        space_recv = lax.ppermute(space_out[1], "head", swap)
+
+        def clamped(whose):
+            return jnp.clip(head_ids - whose * space_count, 0, space_count - 1)
+
+        sources = [(space_out[0], clamped(own_side)), (space_recv, clamped(1 - own_side))]
+        chosen = (head_ids // space_count != own_side).astype(jnp.int32)
+    else:
+        space_all = lax.all_to_all(space_out, "head", 0, 0, tiled=True)
+        sources = [(space_all.reshape(total_heads, part_rows, HD), head_ids)]
+        chosen = jnp.zeros_like(head_ids)
+    all_groups = jnp.arange(sides * groups, dtype=jnp.int32)
+    firsts = 3 * all_groups + jnp.where(slots == 0, 1, 0)
+    seconds = 3 * all_groups + jnp.where(slots == 2, 1, 2)
+    space_columns = jnp.stack([firsts, seconds], axis=1).reshape(total_heads)
+    placed = place_space(space_columns, chosen, sources, sides * groups * 3 * HD)
+
+    if deal == sides:
+        q = pos_count // sides
+        timed = lax.all_to_all(
+            time_out.reshape(frame_count * sides, groups, q, HD), ("frame", "head"), 0, 0, tiled=True
+        )
+        timed = timed.reshape(frame_count, sides, groups, q, HD)
+        block = (frame_count, None, None, q, HD)
+
+        def index(g, t):
+            return (0, g // groups, lax.rem(g, groups), 0, 0)
+
+    else:
+        timed = time_out.reshape(frame_count, groups, pos_count, HD)
+        timed = lax.all_to_all(timed, "frame", 0, 0, tiled=True)
+        timed = lax.all_to_all(timed, "head", 0, 0, tiled=True)
+        timed = timed.reshape(sides, frame_count // sides, groups, pos_count, HD)
+        block = (None, frame_count // sides, None, pos_count, HD)
+
+        def index(g, t):
+            return (g // groups, 0, lax.rem(g, groups), 0, 0)
+
+    return place_time(3 * all_groups + slots, timed, block, index, placed)
 
 
 def solution(mesh):
@@ -460,6 +447,4 @@
         P("head", None, None),
     )
 
-    return jax.shard_map(
-        on_device, mesh=mesh, in_specs=placed, out_specs=P(("frame", "head"), None), check_vma=False
-    )
+    return jax.shard_map(on_device, mesh=mesh, in_specs=placed, out_specs=P(("frame", "head"), None), check_vma=False)

time: 211 us -> 236 us (1.12)
  waiting for transfers between devices: 40.4 us -> 99.2 us
  starting transfers between devices: 44.5 us -> 17.9 us
  Pallas kernels: 109 us -> 100 us
    ppermute x1, waiting for transfers between devices: 11 us -> 67.4 us  [on_device(): prev_kv = lax.ppermute(to_next, 'frame', up)]
    all_to_all x2 -> x1, starting transfers between devices: 21.1 us -> 3.94 us  [on_device(): lax.all_to_all(time_out.reshape(frame_count * sides, groups, q, HD), ('fr...]
    ppermute x4 -> x1, waiting for transfers between devices: 20 us -> 31.8 us  [on_device(): space_recv = lax.ppermute(space_out[1], 'head', swap)]
    pallas_call x2 -> x1, Pallas kernels: 32.3 us -> 22.6 us  [space_attend(): pl.pallas_call(functools.partial(space_attend_kernel, factor, parts), out...]
    all_to_all x2 -> x1, waiting for transfers between devices: 9.41 us -> 0.01 us  [on_device(): lax.all_to_all(time_out.reshape(frame_count * sides, groups, q, HD), ('fr...]
    pallas_call x1 -> x2, Pallas kernels: 7.41 us -> 16.1 us  [the longest x1 10.2 us: place_space(): pl.pallas_call(functools.partial(place_space_kernel, len(sources)), out_s...]
    pallas_call x4 -> x3, Pallas kernels: 57.9 us -> 52.8 us  [project(): pl.pallas_call(functools.partial(project_kernel, kinds, pair, near_count,...]
    all_to_all x2 -> x1, starting transfers between devices: 11.3 us -> 6.32 us  [on_device(): lax.all_to_all(packed, 'frame', split_axis=0, concat_axis=0, tiled=True)]
  transfers between devices with their start and end apart: 11 -> 6, of which waited for: 5 -> 2; matrix products, arithmetic and copies ran while one was open for 6% -> 3% of each run, Pallas kernels for 49% -> 20%
where the time goes in v3:
time: 236 us; the launch traced here: 233 us
  Pallas kernels  100 us (42%)
  waiting for transfers between devices  99.2 us (42%)
  starting transfers between devices  17.9 us (8%)
  local copies, waits for them, and re-layouts  9.29 us (4%)
  other arithmetic  5.89 us (2%)
    ppermute x1, waiting for transfers between devices, on_device(): prev_kv = lax.ppermute(to_next, 'frame', up)  67.4 us
    pallas_call x3, Pallas kernels, project(): pl.pallas_call(functools.partial(project_kernel, kinds, pair, near_count,...  52.8 us
    ppermute x1, waiting for transfers between devices, on_device(): space_recv = lax.ppermute(space_out[1], 'head', swap)  31.8 us
    pallas_call x1, Pallas kernels, space_attend(): pl.pallas_call(functools.partial(space_attend_kernel, factor, parts), out...  22.6 us
    pallas_call x1, Pallas kernels, place_space(): pl.pallas_call(functools.partial(place_space_kernel, len(sources)), out_s...  10.2 us
    pallas_call x1, Pallas kernels, time_attend(): pl.pallas_call(functools.partial(time_attend_kernel, factor, mask.shape[1...  8.54 us
    all_to_all x1, starting transfers between devices, on_device(): lax.all_to_all(packed, 'frame', split_axis=0, concat_axis=0, tiled=True)  6.32 us
    pallas_call x1, Pallas kernels, place_time(): pl.pallas_call(place_time_kernel, out_shape=jax.ShapeDtypeStruct(placed.s...  5.88 us
  transfers between devices with their start and end apart: 6, of which 2 were waited for; matrix products, arithmetic and copies ran while one was open for 3% of the time, Pallas kernels for 20%

profile of v3, /device:TPU:18, one launch (start us, length us, event | category | flops | bytes accessed | tf_op | source)
XLA Modules:
  0.0 232.5 jit_solution(2032899729282425786)
XLA Ops:
  0.0 0.8 reshape.251
  0.8 0.1 multiply_reduce_fusion.6
  0.9 0.1 copy.24
  1.0 0.1 reshape.252.table
  1.1 0.1 reshape.255
  1.2 0.5 multiply_add_fusion.table
  1.7 0.6 gather_fusion.1
  2.3 0.1 copy.27
  2.4 0.1 broadcast_select_fusion
  2.5 0.3 slice_reduce_fusion.1
  2.8 0.1 multiply_reduce_fusion.3
  3.0 0.3 fusion.2
  3.3 0.1 reshape.256
  3.4 0.6 pad_add_fusion.2.table
  4.1 21.7 %shard_map.73 = (bf16[2,8,1024,128]{3,2,1,0:T(8,128)(2,1)}, bf16[2,8,512,128]{3,2,1,0:T(8,128)(2,1)}, bf16[2,8,512,128]{3,2,1,0:T(8,128)(2,1)}) custom-call(s32[136]{0:T(256)} %pad_add_fusion.2.table, bf16[1024,3072]{1,0:T(8,128)(2,1)} %x_ref.5, f32[1,128]{1,0:T(1,128)} %bitcast.27, f32[1,128]{1,0:T(1,128)} %bitcast.31, f32[1,128]{1,0:T(1,128)} %bitcast.28, ...), custom_call_target="tpu_custom_call" | custom-call | flops 12884901888 | bytes 23068672 | tf_op jit(solution)/shard_map/pallas_call | solution.py:101
  25.8 17.4 %shard_map.74.after_ref = bf16[16,3,4,64,128]{4,3,2,1,0:T(8,128)(2,1)} custom-call(s32[4]{0:T(128)} %multiply_add_fusion.table, bf16[1024,3072]{1,0:T(8,128)(2,1)} %x_ref.5, f32[1,128]{1,0:T(1,128)} %bitcast.29, f32[1,128]{1,0:T(1,128)} %bitcast.32, bf16[2,8,1024,128]{3,2,1,0:T(8,128)(2,1)} %get-tuple-element.11.after_ref.kv_ref, ...), custom_call_target="tpu_custom_call" | custom-call | flops 9663676416 | bytes 18874368 | tf_op jit(solution)/shard_map/pallas_call | solution.py:101
  43.2 6.3 %all-to-all-start = ((bf16[16,3,4,64,128]{4,3,2,1,0:T(8,128)(2,1)}), bf16[16,3,4,64,128]{4,3,2,1,0:T(8,128)(2,1)S(1)}, u32[]{:S(2)}, u32[]{:S(2)}) async-start(bf16[16,3,4,64,128]{4,3,2,1,0:T(8,128)(2,1)} %shard_map.74.after_ref), calls=%async_computation | async-start | bytes 6291456 | tf_op jit(solution)/shard_map/all_to_all | solution.py:373
  49.5 2.0 collective-permute-start.1
  51.6 4.4 %collective-permute-start.2 = (bf16[2,8,512,128]{3,2,1,0:T(8,128)(2,1)}, bf16[2,8,512,128]{3,2,1,0:T(8,128)(2,1)}, u32[]{:S(2)}, u32[]{:S(2)}) collective-permute-start(bf16[2,8,512,128]{3,2,1,0:T(8,128)(2,1)} %get-tuple-element.14), channel_id=1, source_target_pairs={{2,0},{4,2},{6,4},{8,6},{10,8},{12,10},{14,12},{16,14},{18,16},{20... | collective-permute-start | bytes 6291464 | tf_op jit(solution)/shard_map/ppermute | solution.py:371
  56.0 0.6 collective-permute-start
  56.6 0.1 copy.30
  56.7 0.1 copy.29
  56.8 0.0 copy-done.7
  56.8 0.1 copy.25
  56.9 0.6 gather_fusion
  57.5 0.1 broadcast_select_fusion.1
  57.5 0.7 select_n.121.mask
  58.2 1.2 multiply_reduce_fusion
  59.4 1.2 multiply_reduce_fusion.1
  60.6 0.7 pad.4.bias_ref
  61.3 13.6 %shard_map.75.q_ref.after_ref = bf16[1,8,1024,128]{3,2,1,0:T(8,128)(2,1)} custom-call(s32[8]{0:T(128)} %copy-done.6, bf16[1024,3072]{1,0:T(8,128)(2,1)} %x_ref.5, f32[1,128]{1,0:T(1,128)} %bitcast.30, f32[1,128]{1,0:T(1,128)} %bitcast.33, bf16[16,3,4,64,128]{4,3,2,1,0:T(8,128)(2,1)} %shard_map.74.after_ref, bf16[3,3072,1536]{2,1,0:T(8,128)(2,1)} %refs_1_.5, ...), custom_call_target="tpu_custom_call" | custom-call | flops 6442450944 | bytes 14680064 | tf_op jit(solution)/shard_map/pallas_call | solution.py:101
  74.9 67.4 %collective-permute-done.1.prev_ref = bf16[2,8,512,128]{3,2,1,0:T(8,128)(2,1)} collective-permute-done((bf16[2,8,512,128]{3,2,1,0:T(8,128)(2,1)}, bf16[2,8,512,128]{3,2,1,0:T(8,128)(2,1)}, u32[]{:S(2)}, u32[]{:S(2)}) %collective-permute-start.1) | collective-permute-done | bytes 2097184 | tf_op jit(solution)/shard_map/ppermute | solution.py:370
  142.3 22.6 %space_attend.1.after_ref = bf16[2,8,512,128]{3,2,1,0:T(8,128)(2,1)} custom-call(s32[1]{0:T(128)} %bitcast.7.side, bf16[1,8,1024,128]{3,2,1,0:T(8,128)(2,1)} %shard_map.75.q_ref.after_ref, bf16[2,8,1024,128]{3,2,1,0:T(8,128)(2,1)} %get-tuple-element.11.after_ref.kv_ref, bf16[2,8,512,128]{3,2,1,0:T(8,128)(2,1)} %collective-permute-done.1.prev_ref, ...), custom_call_target="tpu_custom_call" | custom-call | flops 17179869184 | bytes 12582912 | tf_op jit(solution)/shard_map/space_attend/pallas_call | solution.py:174
  165.0 1.7 copy-done.3
  166.6 8.5 %time_attend.1 = bf16[16,2,4,32,128]{4,3,2,1,0:T(8,128)(2,1)} custom-call(s32[16]{0:T(128)} %select_n.121.mask, bf16[16,3,4,64,128]{4,3,2,1,0:T(8,128)(2,1)} %copy-done.3, bf16[2,8,512,128]{3,2,1,0:T(8,128)(2,1)} %space_attend.1.after_ref), custom_call_target="tpu_custom_call" | custom-call | flops 4294967296 | bytes 4194304 | tf_op jit(solution)/shard_map/time_attend/pallas_call | solution.py:239
  175.2 3.9 %all-to-all-start.1 = ((bf16[32,4,32,128]{3,2,1,0:T(8,128)(2,1)}), bf16[32,4,32,128]{3,2,1,0:T(8,128)(2,1)S(1)}, u32[]{:S(2)}, u32[]{:S(2)}) async-start(bf16[32,4,32,128]{3,2,1,0:T(8,128)(2,1)} %bitcast.23), calls=%async_computation.1 | async-start | bytes 2097152 | tf_op jit(solution)/shard_map/all_to_all | solution.py:417
  179.1 1.5 slice_bitcast_fusion
  180.6 0.6 collective-permute-start.3
  181.2 0.1 fusion.8
  181.3 0.1 copy.31
  181.4 0.1 reshape.260
  181.5 0.6 fusion.5.table
  182.0 0.6 pad_add_fusion.4.table
  182.6 31.8 %collective-permute-done.3.refs_1_ = bf16[8,512,128]{2,1,0:T(8,128)(2,1)S(1)} collective-permute-done((bf16[8,512,128]{2,1,0:T(8,128)(2,1)}, bf16[8,512,128]{2,1,0:T(8,128)(2,1)S(1)}, u32[]{:S(2)}, u32[]{:S(2)}) %collective-permute-start.3) | collective-permute-done | bytes 1048608 | tf_op jit(solution)/shard_map/ppermute | solution.py:398
  214.4 1.0 copy-done.5
  215.4 10.2 %place_space.1.placed_ref = bf16[512,3072]{1,0:T(8,128)(2,1)} custom-call(s32[64]{0:T(128)} %pad_add_fusion.4.table, bf16[8,512,128]{2,1,0:T(8,128)(2,1)} %get-tuple-element.22.refs_0_, bf16[8,512,128]{2,1,0:T(8,128)(2,1)} %copy-done.5), custom_call_target="tpu_custom_call" | custom-call | bytes 4194304 | tf_op jit(solution)/shard_map/place_space/pallas_call | solution.py:283
  225.7 1.0 copy-done.2
  226.7 5.9 %place_time.1 = bf16[512,3072]{1,0:T(8,128)(2,1)} custom-call(s32[8]{0:T(128)} %fusion.5.table, bf16[16,2,4,32,128]{4,3,2,1,0:T(8,128)(2,1)} %bitcast.22, bf16[512,3072]{1,0:T(8,128)(2,1)} %place_space.1.placed_ref), custom_call_target="tpu_custom_call", output_to_operand_aliasing={{}: (2, {})} | custom-call | bytes 2097152 | tf_op jit(solution)/shard_map/place_time/pallas_call | solution.py:303
  (33 shorter events, 0.2 us)
Async XLA Ops:
  0.0 1.7 copy-start
  1.1 24.7 %copy-start.6 = (s32[8]{0:T(128)}, s32[8]{0:T(128)S(1)}, u32[]{:S(2)}) copy-start(s32[8]{0:T(128)S(1)} %reshape.252.table) | copy-start | bytes 100
  43.2 13.6 %copy-start.7 = (s32[12,2,2]{0,2,1:T(2,128)S(1)}, s32[12,2,2]{0,2,1:T(2,128)}, u32[]{:S(2)}) copy-start(s32[12,2,2]{0,2,1:T(2,128)} %param.13) | copy-start | bytes 580
  43.2 121.7 %all-to-all-start = ((bf16[16,3,4,64,128]{4,3,2,1,0:T(8,128)(2,1)}), bf16[16,3,4,64,128]{4,3,2,1,0:T(8,128)(2,1)S(1)}, u32[]{:S(2)}, u32[]{:S(2)}) async-start(bf16[16,3,4,64,128]{4,3,2,1,0:T(8,128)(2,1)} %shard_map.74.after_ref), calls=%async_computation | async-start | bytes 6291456 | tf_op jit(solution)/shard_map/all_to_all | solution.py:373
  49.5 92.8 %collective-permute-start.1 = (bf16[2,8,512,128]{3,2,1,0:T(8,128)(2,1)}, bf16[2,8,512,128]{3,2,1,0:T(8,128)(2,1)}, u32[]{:S(2)}, u32[]{:S(2)}) collective-permute-start(bf16[2,8,512,128]{3,2,1,0:T(8,128)(2,1)} %get-tuple-element.13), channel_id=1, source_target_pairs={{0,2},{2,4},{4,6},{6,8},{8,10},{10,12},{12,14},{14,16},{16,18},{18... | collective-permute-start | bytes 6291464 | tf_op jit(solution)/shard_map/ppermute | solution.py:370
  51.6 90.8 %collective-permute-start.2 = (bf16[2,8,512,128]{3,2,1,0:T(8,128)(2,1)}, bf16[2,8,512,128]{3,2,1,0:T(8,128)(2,1)}, u32[]{:S(2)}, u32[]{:S(2)}) collective-permute-start(bf16[2,8,512,128]{3,2,1,0:T(8,128)(2,1)} %get-tuple-element.14), channel_id=1, source_target_pairs={{2,0},{4,2},{6,4},{8,6},{10,8},{12,10},{14,12},{16,14},{18,16},{20... | collective-permute-start | bytes 6291464 | tf_op jit(solution)/shard_map/ppermute | solution.py:371
  56.0 5.2 %collective-permute-start = (s32[4]{0:T(128)S(1)}, s32[4]{0:T(128)S(1)}, u32[]{:S(2)}, u32[]{:S(2)}) collective-permute-start(s32[4]{0:T(128)S(1)} %multiply_reduce_fusion.6), channel_id=1, source_target_pairs={{0,1},{1,0},{2,3},{3,2},{4,5},{5,4},{6,7},{7,6},{8,9},{9,8},{10,11... | collective-permute-start | bytes 56 | tf_op jit(solution)/shard_map/ppermute | solution.py:376
  164.9 1.7 copy-start.3
  175.2 4.0 %copy-start.4 = (bf16[2,8,512,128]{3,2,1,0:T(8,128)(2,1)S(1)}, bf16[2,8,512,128]{3,2,1,0:T(8,128)(2,1)}, u32[]{:S(2)}) copy-start(bf16[2,8,512,128]{3,2,1,0:T(8,128)(2,1)} %space_attend.1.after_ref) | copy-start | bytes 6291460
  175.2 50.5 %all-to-all-start.1 = ((bf16[32,4,32,128]{3,2,1,0:T(8,128)(2,1)}), bf16[32,4,32,128]{3,2,1,0:T(8,128)(2,1)S(1)}, u32[]{:S(2)}, u32[]{:S(2)}) async-start(bf16[32,4,32,128]{3,2,1,0:T(8,128)(2,1)} %bitcast.23), calls=%async_computation.1 | async-start | bytes 2097152 | tf_op jit(solution)/shard_map/all_to_all | solution.py:417
  180.6 33.8 %collective-permute-start.3 = (bf16[8,512,128]{2,1,0:T(8,128)(2,1)}, bf16[8,512,128]{2,1,0:T(8,128)(2,1)S(1)}, u32[]{:S(2)}, u32[]{:S(2)}) collective-permute-start(bf16[8,512,128]{2,1,0:T(8,128)(2,1)} %get-tuple-element.21), channel_id=1, source_target_pairs={{0,1},{1,0},{2,3},{3,2},{4,5},{5,4},{6,7},{7,6},{8,9},{9,8},{10,11... | collective-permute-start | bytes 3145736 | tf_op jit(solution)/shard_map/ppermute | solution.py:398
  214.4 1.0 copy-start.5
  225.7 1.0 copy-start.2
  225.7 6.9 %copy-start.1 = (s32[12,16,48]{2,1,0:T(8,128)S(1)}, s32[12,16,48]{2,1,0:T(8,128)}, u32[]{:S(2)}) copy-start(s32[12,16,48]{2,1,0:T(8,128)} %param.12) | copy-start | bytes 110596

commit v4 on v3

--- a/solution.py
+++ b/solution.py
@@ -294,24 +294,40 @@
     )(jnp.concatenate([columns, chosen] + [at for _, at in sources]), *[array for array, _ in sources])
 
 
-def place_time_kernel(table, timed_ref, placed_ref, out_ref):
-    out_ref[...] = timed_ref[...].reshape(out_ref.shape)
-
-
-def place_time(columns, timed, block, index, placed):
+def place_time_kernel(pick, count, table, timed_ref, placed_ref, out_ref, held, sems):
+    copies = []
+    for g in range(count):
+        held[g] = pick(timed_ref, g).reshape(held.shape[1:])
+        column = pl.ds(pl.multiple_of(table[g] * HD, HD), HD)
+        copies.append(pltpu.make_async_copy(held.at[g], out_ref.at[:, column], sems.at[g]))
+        copies[-1].start()
+    for copy in copies:
+        copy.wait()
+
+
+def place_time(columns, timed, pick, placed):
     rows = placed.shape[0]
+    count = columns.shape[0]
     return pl.pallas_call(
-        place_time_kernel,
+        functools.partial(place_time_kernel, pick, count),
         out_shape=jax.ShapeDtypeStruct(placed.shape, placed.dtype),
         grid_spec=pltpu.PrefetchScalarGridSpec(
             num_scalar_prefetch=1,
-            grid=(columns.shape[0],),
-            in_specs=[pl.BlockSpec(block, index), pl.BlockSpec(memory_space=pl.ANY)],
-            out_specs=pl.BlockSpec((rows, HD), lambda g, t: (0, t[g])),
+            grid=(1,),
+            in_specs=[
+                pl.BlockSpec(memory_space=pltpu.VMEM),
+                pl.BlockSpec(memory_space=pl.ANY),
+            ],
+            out_specs=pl.BlockSpec(memory_space=pl.ANY),
+            scratch_shapes=[
+                pltpu.VMEM((count, rows, HD), jnp.bfloat16),
+                pltpu.SemaphoreType.DMA((count,)),
+            ],
         ),
         input_output_aliases={2: 0},
+        compiler_params=pltpu.CompilerParams(vmem_limit_bytes=16 * 1024 * 1024),
         cost_estimate=pl.CostEstimate(
-            flops=0, bytes_accessed=4 * rows * columns.shape[0] * HD, transcendentals=0
+            flops=0, bytes_accessed=4 * rows * count * HD, transcendentals=0
         ),
         name="place_time",
     )(columns, timed, placed)
@@ -418,22 +434,20 @@
             time_out.reshape(frame_count * sides, groups, q, HD), ("frame", "head"), 0, 0, tiled=True
         )
         timed = timed.reshape(frame_count, sides, groups, q, HD)
-        block = (frame_count, None, None, q, HD)
-
-        def index(g, t):
-            return (0, g // groups, lax.rem(g, groups), 0, 0)
+
+        def pick(ref, g):
+            return ref[:, g // groups, g % groups]
 
     else:
         timed = time_out.reshape(frame_count, groups, pos_count, HD)
         timed = lax.all_to_all(timed, "frame", 0, 0, tiled=True)
         timed = lax.all_to_all(timed, "head", 0, 0, tiled=True)
         timed = timed.reshape(sides, frame_count // sides, groups, pos_count, HD)
-        block = (None, frame_count // sides, None, pos_count, HD)
-
-        def index(g, t):
-            return (g // groups, 0, lax.rem(g, groups), 0, 0)
-
-    return place_time(3 * all_groups + slots, timed, block, index, placed)
+
+        def pick(ref, g):
+            return ref[g // groups, :, g % groups]
+
+    return place_time(3 * all_groups + slots, timed, pick, placed)
 
 
 def solution(mesh):

time: 236 us -> 230 us (0.975)
  Pallas kernels: 100 us -> 95.8 us
    pallas_call x1, Pallas kernels: 5.88 us -> 1.57 us  [place_time(): pl.pallas_call(functools.partial(place_time_kernel, pick, count), out_sha...]
where the time goes in v4:
time: 230 us; the launch traced here: 227 us
  waiting for transfers between devices  99.7 us (43%)
  Pallas kernels  95.8 us (42%)
  starting transfers between devices  17.9 us (8%)
  local copies, waits for them, and re-layouts  8.31 us (4%)
  other arithmetic  5.37 us (2%)
    ppermute x1, waiting for transfers between devices, on_device(): prev_kv = lax.ppermute(to_next, 'frame', up)  67.4 us
    pallas_call x3, Pallas kernels, project(): pl.pallas_call(functools.partial(project_kernel, kinds, pair, near_count,...  52.8 us
    ppermute x1, waiting for transfers between devices, on_device(): space_recv = lax.ppermute(space_out[1], 'head', swap)  32.3 us
    pallas_call x1, Pallas kernels, space_attend(): pl.pallas_call(functools.partial(space_attend_kernel, factor, parts), out...  22.6 us
    pallas_call x1, Pallas kernels, place_space(): pl.pallas_call(functools.partial(place_space_kernel, len(sources)), out_s...  10.2 us
    pallas_call x1, Pallas kernels, time_attend(): pl.pallas_call(functools.partial(time_attend_kernel, factor, mask.shape[1...  8.54 us
    all_to_all x1, starting transfers between devices, on_device(): lax.all_to_all(packed, 'frame', split_axis=0, concat_axis=0, tiled=True)  6.32 us
  transfers between devices with their start and end apart: 6, of which 2 were waited for; matrix products, arithmetic and copies ran while one was open for 3% of the time, Pallas kernels for 20%

profile of v4, /device:TPU:18, one launch (start us, length us, event | category | flops | bytes accessed | tf_op | source)
XLA Modules:
  0.0 227.3 jit_solution(2405814364990873385)
XLA Ops:
  0.0 0.8 reshape.251
  0.8 0.1 multiply_reduce_fusion.6
  0.9 0.1 copy.24
  1.0 0.1 reshape.252.table
  1.1 0.1 reshape.255
  1.2 0.5 multiply_add_fusion.table
  1.7 0.6 gather_fusion.1
  2.3 0.1 copy.27
  2.4 0.1 broadcast_select_fusion
  2.5 0.3 slice_reduce_fusion.1
  2.8 0.1 multiply_reduce_fusion.3
  3.0 0.3 fusion.2
  3.3 0.1 reshape.256
  3.4 0.6 pad_add_fusion.2.table
  4.1 21.7 %shard_map.73 = (bf16[2,8,1024,128]{3,2,1,0:T(8,128)(2,1)}, bf16[2,8,512,128]{3,2,1,0:T(8,128)(2,1)}, bf16[2,8,512,128]{3,2,1,0:T(8,128)(2,1)}) custom-call(s32[136]{0:T(256)} %pad_add_fusion.2.table, bf16[1024,3072]{1,0:T(8,128)(2,1)} %x_ref.5, f32[1,128]{1,0:T(1,128)} %bitcast.27, f32[1,128]{1,0:T(1,128)} %bitcast.31, f32[1,128]{1,0:T(1,128)} %bitcast.28, ...), custom_call_target="tpu_custom_call" | custom-call | flops 12884901888 | bytes 23068672 | tf_op jit(solution)/shard_map/pallas_call | solution.py:101
  25.8 17.4 %shard_map.74.after_ref = bf16[16,3,4,64,128]{4,3,2,1,0:T(8,128)(2,1)} custom-call(s32[4]{0:T(128)} %multiply_add_fusion.table, bf16[1024,3072]{1,0:T(8,128)(2,1)} %x_ref.5, f32[1,128]{1,0:T(1,128)} %bitcast.29, f32[1,128]{1,0:T(1,128)} %bitcast.32, bf16[2,8,1024,128]{3,2,1,0:T(8,128)(2,1)} %get-tuple-element.11.after_ref.kv_ref, ...), custom_call_target="tpu_custom_call" | custom-call | flops 9663676416 | bytes 18874368 | tf_op jit(solution)/shard_map/pallas_call | solution.py:101
  43.2 6.3 %all-to-all-start = ((bf16[16,3,4,64,128]{4,3,2,1,0:T(8,128)(2,1)}), bf16[16,3,4,64,128]{4,3,2,1,0:T(8,128)(2,1)S(1)}, u32[]{:S(2)}, u32[]{:S(2)}) async-start(bf16[16,3,4,64,128]{4,3,2,1,0:T(8,128)(2,1)} %shard_map.74.after_ref), calls=%async_computation | async-start | bytes 6291456 | tf_op jit(solution)/shard_map/all_to_all | solution.py:389
  49.5 2.0 collective-permute-start.1
  51.6 4.4 %collective-permute-start.2 = (bf16[2,8,512,128]{3,2,1,0:T(8,128)(2,1)}, bf16[2,8,512,128]{3,2,1,0:T(8,128)(2,1)}, u32[]{:S(2)}, u32[]{:S(2)}) collective-permute-start(bf16[2,8,512,128]{3,2,1,0:T(8,128)(2,1)} %get-tuple-element.14), channel_id=1, source_target_pairs={{2,0},{4,2},{6,4},{8,6},{10,8},{12,10},{14,12},{16,14},{18,16},{20... | collective-permute-start | bytes 6291464 | tf_op jit(solution)/shard_map/ppermute | solution.py:387
  56.0 0.6 collective-permute-start
  56.6 0.1 copy.30
  56.7 0.1 copy.29
  56.8 0.0 copy-done.6
  56.8 0.1 copy.25
  56.9 0.6 gather_fusion
  57.5 0.1 broadcast_select_fusion.1
  57.5 0.7 select_n.121.mask
  58.2 1.2 multiply_reduce_fusion
  59.4 1.2 multiply_reduce_fusion.1
  60.6 0.7 pad.4.bias_ref
  61.3 0.0 collective-permute-done
  61.3 13.6 %shard_map.75.q_ref.after_ref = bf16[1,8,1024,128]{3,2,1,0:T(8,128)(2,1)} custom-call(s32[8]{0:T(128)} %copy-done.5, bf16[1024,3072]{1,0:T(8,128)(2,1)} %x_ref.5, f32[1,128]{1,0:T(1,128)} %bitcast.30, f32[1,128]{1,0:T(1,128)} %bitcast.33, bf16[16,3,4,64,128]{4,3,2,1,0:T(8,128)(2,1)} %shard_map.74.after_ref, bf16[3,3072,1536]{2,1,0:T(8,128)(2,1)} %refs_1_.5, ...), custom_call_target="tpu_custom_call" | custom-call | flops 6442450944 | bytes 14680064 | tf_op jit(solution)/shard_map/pallas_call | solution.py:101
  74.9 67.4 %collective-permute-done.1.prev_ref = bf16[2,8,512,128]{3,2,1,0:T(8,128)(2,1)} collective-permute-done((bf16[2,8,512,128]{3,2,1,0:T(8,128)(2,1)}, bf16[2,8,512,128]{3,2,1,0:T(8,128)(2,1)}, u32[]{:S(2)}, u32[]{:S(2)}) %collective-permute-start.1) | collective-permute-done | bytes 2097184 | tf_op jit(solution)/shard_map/ppermute | solution.py:386
  142.3 22.6 %space_attend.1.after_ref = bf16[2,8,512,128]{3,2,1,0:T(8,128)(2,1)} custom-call(s32[1]{0:T(128)} %bitcast.7.side, bf16[1,8,1024,128]{3,2,1,0:T(8,128)(2,1)} %shard_map.75.q_ref.after_ref, bf16[2,8,1024,128]{3,2,1,0:T(8,128)(2,1)} %get-tuple-element.11.after_ref.kv_ref, bf16[2,8,512,128]{3,2,1,0:T(8,128)(2,1)} %collective-permute-done.1.prev_ref, ...), custom_call_target="tpu_custom_call" | custom-call | flops 17179869184 | bytes 12582912 | tf_op jit(solution)/shard_map/space_attend/pallas_call | solution.py:174
  165.0 1.7 copy-done.2
  166.6 8.5 %time_attend.1 = bf16[16,2,4,32,128]{4,3,2,1,0:T(8,128)(2,1)} custom-call(s32[16]{0:T(128)} %select_n.121.mask, bf16[16,3,4,64,128]{4,3,2,1,0:T(8,128)(2,1)} %copy-done.2, bf16[2,8,512,128]{3,2,1,0:T(8,128)(2,1)} %space_attend.1.after_ref), custom_call_target="tpu_custom_call" | custom-call | flops 4294967296 | bytes 4194304 | tf_op jit(solution)/shard_map/time_attend/pallas_call | solution.py:239
  175.2 3.9 %all-to-all-start.1 = ((bf16[32,4,32,128]{3,2,1,0:T(8,128)(2,1)}), bf16[32,4,32,128]{3,2,1,0:T(8,128)(2,1)S(1)}, u32[]{:S(2)}, u32[]{:S(2)}) async-start(bf16[32,4,32,128]{3,2,1,0:T(8,128)(2,1)} %bitcast.23), calls=%async_computation.1 | async-start | bytes 2097152 | tf_op jit(solution)/shard_map/all_to_all | solution.py:433
  179.1 1.5 slice_bitcast_fusion
  180.6 0.6 collective-permute-start.3
  181.2 0.1 fusion.8
  181.3 0.1 copy.31
  181.4 0.1 reshape.260
  181.5 0.1 fusion.5.table
  181.6 0.6 pad_add_fusion.4.table
  182.1 32.3 %collective-permute-done.3.refs_1_ = bf16[8,512,128]{2,1,0:T(8,128)(2,1)S(1)} collective-permute-done((bf16[8,512,128]{2,1,0:T(8,128)(2,1)}, bf16[8,512,128]{2,1,0:T(8,128)(2,1)S(1)}, u32[]{:S(2)}, u32[]{:S(2)}) %collective-permute-start.3) | collective-permute-done | bytes 1048608 | tf_op jit(solution)/shard_map/ppermute | solution.py:414
  214.4 1.0 copy-done.4
  215.4 10.2 %place_space.1.placed_ref = bf16[512,3072]{1,0:T(8,128)(2,1)} custom-call(s32[64]{0:T(128)} %pad_add_fusion.4.table, bf16[8,512,128]{2,1,0:T(8,128)(2,1)} %get-tuple-element.22.refs_0_, bf16[8,512,128]{2,1,0:T(8,128)(2,1)} %copy-done.4), custom_call_target="tpu_custom_call" | custom-call | bytes 4194304 | tf_op jit(solution)/shard_map/place_space/pallas_call | solution.py:283
  225.7 1.6 place_time.1
  (31 shorter events, 0.2 us)
Async XLA Ops:
  0.0 1.7 copy-start
  1.1 24.7 %copy-start.5 = (s32[8]{0:T(128)}, s32[8]{0:T(128)S(1)}, u32[]{:S(2)}) copy-start(s32[8]{0:T(128)S(1)} %reshape.252.table) | copy-start | bytes 100
  43.2 13.6 %copy-start.6 = (s32[12,2,2]{0,2,1:T(2,128)S(1)}, s32[12,2,2]{0,2,1:T(2,128)}, u32[]{:S(2)}) copy-start(s32[12,2,2]{0,2,1:T(2,128)} %param.13) | copy-start | bytes 580
  43.2 121.7 %all-to-all-start = ((bf16[16,3,4,64,128]{4,3,2,1,0:T(8,128)(2,1)}), bf16[16,3,4,64,128]{4,3,2,1,0:T(8,128)(2,1)S(1)}, u32[]{:S(2)}, u32[]{:S(2)}) async-start(bf16[16,3,4,64,128]{4,3,2,1,0:T(8,128)(2,1)} %shard_map.74.after_ref), calls=%async_computation | async-start | bytes 6291456 | tf_op jit(solution)/shard_map/all_to_all | solution.py:389
  49.5 92.8 %collective-permute-start.1 = (bf16[2,8,512,128]{3,2,1,0:T(8,128)(2,1)}, bf16[2,8,512,128]{3,2,1,0:T(8,128)(2,1)}, u32[]{:S(2)}, u32[]{:S(2)}) collective-permute-start(bf16[2,8,512,128]{3,2,1,0:T(8,128)(2,1)} %get-tuple-element.13), channel_id=1, source_target_pairs={{0,2},{2,4},{4,6},{6,8},{8,10},{10,12},{12,14},{14,16},{16,18},{18... | collective-permute-start | bytes 6291464 | tf_op jit(solution)/shard_map/ppermute | solution.py:386
  51.6 90.8 %collective-permute-start.2 = (bf16[2,8,512,128]{3,2,1,0:T(8,128)(2,1)}, bf16[2,8,512,128]{3,2,1,0:T(8,128)(2,1)}, u32[]{:S(2)}, u32[]{:S(2)}) collective-permute-start(bf16[2,8,512,128]{3,2,1,0:T(8,128)(2,1)} %get-tuple-element.14), channel_id=1, source_target_pairs={{2,0},{4,2},{6,4},{8,6},{10,8},{12,10},{14,12},{16,14},{18,16},{20... | collective-permute-start | bytes 6291464 | tf_op jit(solution)/shard_map/ppermute | solution.py:387
  56.0 5.2 %collective-permute-start = (s32[4]{0:T(128)S(1)}, s32[4]{0:T(128)S(1)}, u32[]{:S(2)}, u32[]{:S(2)}) collective-permute-start(s32[4]{0:T(128)S(1)} %multiply_reduce_fusion.6), channel_id=1, source_target_pairs={{0,1},{1,0},{2,3},{3,2},{4,5},{5,4},{6,7},{7,6},{8,9},{9,8},{10,11... | collective-permute-start | bytes 56 | tf_op jit(solution)/shard_map/ppermute | solution.py:392
  164.9 1.7 copy-start.2
  175.2 4.0 %copy-start.3 = (bf16[2,8,512,128]{3,2,1,0:T(8,128)(2,1)S(1)}, bf16[2,8,512,128]{3,2,1,0:T(8,128)(2,1)}, u32[]{:S(2)}) copy-start(bf16[2,8,512,128]{3,2,1,0:T(8,128)(2,1)} %space_attend.1.after_ref) | copy-start | bytes 6291460
  175.2 50.5 %all-to-all-start.1 = ((bf16[32,4,32,128]{3,2,1,0:T(8,128)(2,1)}), bf16[32,4,32,128]{3,2,1,0:T(8,128)(2,1)S(1)}, u32[]{:S(2)}, u32[]{:S(2)}) async-start(bf16[32,4,32,128]{3,2,1,0:T(8,128)(2,1)} %bitcast.23), calls=%async_computation.1 | async-start | bytes 2097152 | tf_op jit(solution)/shard_map/all_to_all | solution.py:433
  180.6 33.8 %collective-permute-start.3 = (bf16[8,512,128]{2,1,0:T(8,128)(2,1)}, bf16[8,512,128]{2,1,0:T(8,128)(2,1)S(1)}, u32[]{:S(2)}, u32[]{:S(2)}) collective-permute-start(bf16[8,512,128]{2,1,0:T(8,128)(2,1)} %get-tuple-element.21), channel_id=1, source_target_pairs={{0,1},{1,0},{2,3},{3,2},{4,5},{5,4},{6,7},{7,6},{8,9},{9,8},{10,11... | collective-permute-start | bytes 3145736 | tf_op jit(solution)/shard_map/ppermute | solution.py:414
  214.4 1.0 copy-start.4
  225.7 1.6 copy-start.1
